TPU v7x, 128 devices: a whole 4x4x4 slice. The times are simulated.
128 devices in a mesh: post: 16 (over z, y), sub: 8 (over x, core).
Axes of the slice: x: 4, y: 4, z: 4, core: 2. Of those that a mesh axis runs over, the one named last changes fastest.
Arguments:
- vectors: bfloat16 [4096, 4096], P(('post', 'sub')), may hold values from -6 to 6
- owner_group_index: int32 [4096, 8], P(('post', 'sub')), may hold values from 0 to 15, all different within a row; in each aligned block of 32 rows (0 to 31, 32 to 63, ...) at most 24 rows name the same one
- local_posting_index: int32 [4096, 8], P(('post', 'sub')), may hold values from 0 to 8191
- slot_valid_mask: int32 [4096, 8], P(('post', 'sub')), may hold values 0 or 1
- slot_posting_weight: bfloat16 [4096, 8], P(('post', 'sub')), may hold values from 0.099609375 to 1
- centroids: bfloat16 [131072, 4096], P('post', 'sub'), may hold values from -4.1875 to 4.1875
- codebook: float32 [64, 256, 64], P('sub'), may hold values from -4.2 to 4.2
- variance: float32 [64], P('sub'), may hold values from 0.5 to 4
Outputs:
- trained_codebook: float32 [64, 256, 64], P('sub')
- slot_quant_error: float32 [4096, 8], P(('post', 'sub'))
Inputs may be any that keep to these rules, and one draw needn't show every extreme that they name: `owner_group_index`: each row names 8 different owners. Within the rows of one device (aligned blocks of 32 rows) no owner is named by more than 24 slots, and in some blocks one owner is named by exactly 24.
All inputs are finite; a program needn't handle non-finite values. No bound on the sum of `slot_valid_mask` on one device may be relied on, other than what follows from the above.
Results may differ from a plain program's by a relative error of at most 0.0004.
Values may be sent and summed in bfloat16 or wider, within the bound.
No kernel may reach another device: no remote copies, remote signals or barrier semaphores. Data moves between devices by JAX's collectives and lax.ppermute only.
A program may use at most 128 MiB of HBM per device.

v0:
```python
import jax
import jax.numpy as jnp
from jax import lax
from jax.sharding import PartitionSpec as P

ITERS = 2


def expect(resid, words, spread, weight):
    cross = jnp.dot(
        resid, words.T, precision=lax.Precision.HIGHEST, preferred_element_type=jnp.float32
    )
    dist = (
        jnp.sum(resid * resid, axis=1)[:, None]
        - 2.0 * cross
        + jnp.sum(words * words, axis=1)[None, :]
    )
    score = -dist / (2.0 * spread)
    top_score = jnp.max(score, axis=1, keepdims=True)
    expval = jnp.exp(score - top_score)
    resp = expval / jnp.sum(expval, axis=1, keepdims=True)
    weighted = resp * weight[:, None]
    sums = jnp.dot(
        weighted.T, resid, precision=lax.Precision.HIGHEST, preferred_element_type=jnp.float32
    )
    counts = jnp.sum(weighted, axis=0)
    error = jnp.sum(resp * dist, axis=1)
    return (sums, counts, error)


def per_device(
    vectors,
    owner_group_index,
    local_posting_index,
    slot_valid_mask,
    slot_posting_weight,
    centroids,
    codebook,
    variance,
):
    posting_count = lax.axis_size("post")
    n_sub = lax.axis_size("sub")
    row_count, slots_per_row = owner_group_index.shape
    vector_width = vectors.shape[1]
    dim_sub = vector_width // n_sub
    slot_capacity = min(row_count, row_count * slots_per_row * 3 // (2 * posting_count))
    slot_count = row_count * slots_per_row
    owner_flattened = owner_group_index.reshape(slot_count)
    member = (
        owner_flattened[:, None] == jnp.arange(posting_count, dtype=jnp.int32)[None, :]
    ).astype(jnp.int32)
    rank = jnp.sum(jnp.cumsum(member, axis=0) * member, axis=1) - 1
    target = owner_flattened * slot_capacity + rank
    source_rows = (
        jnp.full((posting_count * slot_capacity,), slot_count, jnp.int32)
        .at[target]
        .set(jnp.arange(slot_count, dtype=jnp.int32))
    )
    filled_slots = source_rows < slot_count
    safe_index = jnp.minimum(source_rows, slot_count - 1)
    packed = jnp.where(
        filled_slots[:, None], vectors[safe_index // slots_per_row], jnp.zeros((), vectors.dtype)
    )
    packed_local_index = jnp.where(
        filled_slots, local_posting_index.reshape(slot_count)[safe_index], 0
    )
    weight_masked = slot_posting_weight * slot_valid_mask.astype(slot_posting_weight.dtype)
    packed_weight = jnp.where(
        filled_slots,
        weight_masked.reshape(slot_count)[safe_index],
        jnp.zeros((), slot_posting_weight.dtype),
    )
    blocks = packed.reshape(posting_count, slot_capacity, n_sub, dim_sub).transpose(0, 2, 1, 3)
    id_blocks = jnp.broadcast_to(
        packed_local_index.reshape(posting_count, 1, slot_capacity),
        (posting_count, n_sub, slot_capacity),
    )
    weight_blocks = jnp.broadcast_to(
        packed_weight.reshape(posting_count, 1, slot_capacity),
        (posting_count, n_sub, slot_capacity),
    )
    data = lax.all_to_all(
        blocks.reshape(posting_count * n_sub, slot_capacity, dim_sub),
        ("post", "sub"),
        split_axis=0,
        concat_axis=0,
        tiled=True,
    )
    ids = lax.all_to_all(
        id_blocks.reshape(posting_count * n_sub, slot_capacity),
        ("post", "sub"),
        split_axis=0,
        concat_axis=0,
        tiled=True,
    )
    weights = lax.all_to_all(
        weight_blocks.reshape(posting_count * n_sub, slot_capacity),
        ("post", "sub"),
        split_axis=0,
        concat_axis=0,
        tiled=True,
    )
    nearest = centroids[ids]
    resid = data.astype(jnp.float32) - nearest.astype(jnp.float32)
    weight = weights.astype(jnp.float32)
    total_slots = posting_count * n_sub * slot_capacity
    local_subs = codebook.shape[0]
    sub_dim = codebook.shape[2]
    resid = resid.reshape(total_slots, local_subs, sub_dim).transpose(1, 0, 2)
    weight = weight.reshape(total_slots)

    def one_sub(packet):
        part, book, spread = packet
        return expect(part, book, spread, weight)

    words = codebook
    errors = jnp.zeros((local_subs, total_slots), jnp.float32)
    for step in range(ITERS):
        sums, counts, errors = lax.map(one_sub, (resid, words, variance))
        sums, counts = lax.psum((sums, counts), "post")
        words = (sums + words) / (counts[:, :, None] + 1.0)
    partial_error = jnp.sum(errors, axis=0)
    returned = lax.all_to_all(
        partial_error.reshape(posting_count * n_sub, slot_capacity),
        ("post", "sub"),
        split_axis=0,
        concat_axis=0,
        tiled=True,
    )
    per_owner = jnp.sum(returned.reshape(posting_count, n_sub, slot_capacity), axis=1)
    slot_value_rows = per_owner.reshape(posting_count * slot_capacity)[target]
    slot_quant_error = (
        slot_value_rows / vector_width * slot_valid_mask.reshape(slot_count).astype(jnp.float32)
    )
    return (words, slot_quant_error.reshape(row_count, slots_per_row))


def solution(mesh):
    in_specs = (
        P(("post", "sub"), None),
        P(("post", "sub"), None),
        P(("post", "sub"), None),
        P(("post", "sub"), None),
        P(("post", "sub"), None),
        P("post", "sub"),
        P("sub", None, None),
        P("sub"),
    )
    out_specs = (P("sub", None, None), P(("post", "sub"), None))
    return jax.shard_map(
        per_device, mesh=mesh, in_specs=in_specs, out_specs=out_specs, check_vma=False
    )
```

profile of v0, /device:TPU:8, one launch (start us, length us, event | category | flops | bytes accessed | tf_op | source)
XLA Modules:
  0.0 609.7 jit_solution(7946779011977939552)
XLA Ops:
  15.8 10.4 %all-to-all-start.2 = ((bf16[128,1,24]{2,1,0:T(2,128)(2,1)}), bf16[128,1,24]{2,1,0:T(2,128)(2,1)S(1)}, u32[]{:S(2)}, u32[]{:S(2)}) async-start(bf16[128,1,24]{2,1,0:T(2,128)(2,1)} %copy.30), calls=%async_computation.2 | async-start | bytes 131072 | tf_op jit(solution)/shard_map/all_to_all | solution.py:96
  37.2 9.8 %all-to-all-start.1 = ((s32[128,1,24]{2,1,0:T(1,128)}), s32[128,1,24]{2,1,0:T(1,128)S(1)}, u32[]{:S(2)}, u32[]{:S(2)}) async-start(s32[128,1,24]{2,1,0:T(1,128)} %bitcast.16), calls=%async_computation.1 | async-start | bytes 131072 | tf_op jit(solution)/shard_map/all_to_all | solution.py:89
  47.0 4.6 copy_select_fusion
  55.8 5.9 all-to-all-start
  62.3 15.7 %gather_fusion.2 = bf16[3072,512]{1,0:T(8,128)(2,1)S(1)} fusion(bf16[8192,512]{1,0:T(8,128)(2,1)} %param.17, s32[3072]{0:T(1024)S(1)} %broadcast_clamp_fusion), kind=kCustom, calls=%fused_computation.2 | custom fusion | bytes 6303744 | tf_op jit(solution)/shard_map/gather | solution.py:103
  78.0 24.1 %all-to-all-done = bf16[128,24,512]{2,1,0:T(8,128)(2,1)} async-done(((bf16[128,24,512]{2,1,0:T(8,128)(2,1)}), bf16[128,24,512]{2,1,0:T(8,128)(2,1)}, u32[]{:S(2)}, u32[]{:S(2)}) %all-to-all-start) | async-done | bytes 3145760 | tf_op jit(solution)/shard_map/all_to_all | solution.py:82
  102.1 5.5 convert_subtract_fusion
  107.5 10.3 %reshape.154 = f32[3072,8,64]{2,1,0:T(8,128)} reshape(f32[128,24,512]{2,1,0:T(8,128)} %convert_subtract_fusion) | data formatting | bytes 12582912 | tf_op jit(solution)/shard_map/reshape | solution.py:109
  117.8 11.6 %copy.32 = f32[8,3072,64]{2,1,0:T(8,128)} copy(f32[8,3072,64]{2,0,1:T(8,128)} %bitcast.146) | data formatting | bytes 12582912 | tf_op jit(solution)/shard_map/while | solution.py:119
  130.2 119.1 %while.28 = (s32[]{:T(128)}, f32[8,256,64]{1,2,0:T(8,128)}, f32[8,256]{1,0:T(8,128)S(1)}, f32[8,3072,64]{2,1,0:T(8,128)}, f32[8,256,64]{1,2,0:T(8,128)}, /*index...) while((s32[]{:T(128)}, f32[8,256,64]{1,2,0:T(8,128)}, ...), condition=%wide.wide.region_10.11_spmd, body=%wide.wide.region_4.10_spmd.sunk | while | flops 1220172288 | bytes 16854672 | solution.py:119
  134.2 4.6 fusion.90
  140.1 5.1 fusion.92
  149.1 4.6 fusion.90
  154.9 5.1 fusion.92
  164.0 4.6 fusion.90
  169.8 5.1 fusion.92
  178.9 4.6 fusion.90
  184.7 5.1 fusion.92
  193.8 4.6 fusion.90
  199.6 5.1 fusion.92
  208.7 4.6 fusion.90
  214.5 5.1 fusion.92
  223.5 4.6 fusion.90
  229.4 5.1 fusion.92
  238.4 4.6 fusion.90
  244.3 5.1 fusion.92
  250.4 38.1 %psum.29 = f32[8,256]{1,0:T(8,128)S(1)} all-reduce(f32[8,256]{1,0:T(8,128)S(1)} %get-tuple-element.85), channel_id=1, replica_groups=mesh['post'=16,'sub'=8] {'post'}, use_global_device_ids=true, to_apply=%region_12.13 | all-reduce | flops 2048 | bytes 16384 | tf_op jit(solution)/shard_map/psum | solution.py:120
  288.5 42.8 %all-reduce.3.cloned.1.call-done = f32[8,256,64]{1,2,0:T(8,128)} async-done(((f32[8,256,64]{1,2,0:T(8,128)}), f32[8,256,64]{1,2,0:T(8,128)}) %all-reduce.3.cloned.1.call-update) | async-done | bytes 524304 | tf_op jit(solution)/shard_map/psum | solution.py:120
  334.3 130.5 %while.29 = (s32[]{:T(128)}, f32[8,256,64]{1,2,0:T(8,128)}, f32[8,256]{1,0:T(8,128)S(1)}, f32[8,3072]{1,0:T(8,128)S(1)}, f32[8,3072,64]{2,1,0:T(8,128)}, /*index...) while((s32[]{:T(128)}, f32[8,256,64]{1,2,0:T(8,128)}, ...), condition=%wide.wide.region_20.21_spmd, body=%wide.wide.region_13.20_spmd.sunk | while | flops 1226460672 | bytes 17154212 | solution.py:119
  338.5 4.6 fusion.98
  345.3 5.3 fusion.100
  354.8 4.6 fusion.98
  361.6 5.3 fusion.100
  371.1 4.6 fusion.98
  377.9 5.3 fusion.100
  387.4 4.6 fusion.98
  394.3 5.3 fusion.100
  403.7 4.6 fusion.98
  410.6 5.3 fusion.100
  420.1 4.6 fusion.98
  426.9 5.3 fusion.100
  436.4 4.6 fusion.98
  443.2 5.3 fusion.100
  459.5 5.3 fusion.100
  464.8 37.1 %psum.31 = f32[8,256]{1,0:T(8,128)S(1)} all-reduce(f32[8,256]{1,0:T(8,128)S(1)} %get-tuple-element.87), channel_id=1, replica_groups=mesh['post'=16,'sub'=8] {'post'}, use_global_device_ids=true, to_apply=%region_22.23 | all-reduce | flops 2048 | bytes 16384 | tf_op jit(solution)/shard_map/psum | solution.py:120
  502.6 6.6 %all-to-all-start.3 = ((f32[128,1,24]{2,1,0:T(1,128)}), f32[128,1,24]{2,1,0:T(1,128)S(1)}, u32[]{:S(2)}, u32[]{:S(2)}) async-start(f32[128,1,24]{2,1,0:T(1,128)} %bitcast.22), calls=%async_computation.3 | async-start | bytes 131072 | tf_op jit(solution)/shard_map/all_to_all | solution.py:123
  510.0 8.2 %all-to-all-done.3 = f32[128,1,24]{2,1,0:T(1,128)S(1)} async-done(((f32[128,1,24]{2,1,0:T(1,128)}), f32[128,1,24]{2,1,0:T(1,128)S(1)}, u32[]{:S(2)}, u32[]{:S(2)}) %all-to-all-start.3) | async-done | bytes 12320 | tf_op jit(solution)/shard_map/all_to_all | solution.py:123
  521.0 79.8 %all-reduce.5.cloned.1.call-done = f32[8,256,64]{1,2,0:T(8,128)} async-done(((f32[8,256,64]{1,2,0:T(8,128)}), f32[8,256,64]{1,2,0:T(8,128)}) %all-reduce.5.cloned.1.call-update) | async-done | bytes 524304 | tf_op jit(solution)/shard_map/psum | solution.py:120
  (198 shorter events, 123.0 us)
Async XLA Ops:
  7.2 23.0 %copy-start = (bf16[32,4096]{1,0:T(8,128)(2,1)S(1)}, bf16[32,4096]{1,0:T(8,128)(2,1)}, u32[]{:S(2)}) copy-start(bf16[32,4096]{1,0:T(8,128)(2,1)} %param.12) | copy-start | bytes 786436
  15.8 20.8 %all-to-all-start.2 = ((bf16[128,1,24]{2,1,0:T(2,128)(2,1)}), bf16[128,1,24]{2,1,0:T(2,128)(2,1)S(1)}, u32[]{:S(2)}, u32[]{:S(2)}) async-start(bf16[128,1,24]{2,1,0:T(2,128)(2,1)} %copy.30), calls=%async_computation.2 | async-start | bytes 131072 | tf_op jit(solution)/shard_map/all_to_all | solution.py:96
  37.2 18.6 %all-to-all-start.1 = ((s32[128,1,24]{2,1,0:T(1,128)}), s32[128,1,24]{2,1,0:T(1,128)S(1)}, u32[]{:S(2)}, u32[]{:S(2)}) async-start(s32[128,1,24]{2,1,0:T(1,128)} %bitcast.16), calls=%async_computation.1 | async-start | bytes 131072 | tf_op jit(solution)/shard_map/all_to_all | solution.py:89
  55.8 46.2 %all-to-all-start = ((bf16[128,24,512]{2,1,0:T(8,128)(2,1)}), bf16[128,24,512]{2,1,0:T(8,128)(2,1)}, u32[]{:S(2)}, u32[]{:S(2)}) async-start(bf16[128,24,512]{2,1,0:T(8,128)(2,1)} %bitcast.15), calls=%async_computation | async-start | bytes 6291456 | tf_op jit(solution)/shard_map/all_to_all | solution.py:82
  61.8 269.6 %all-reduce.3.cloned.1.call-start = ((), (), s32[]{:S(2)}) async-start(), calls=%async_computation.4 | async-start | bytes 1048576 | tf_op jit(solution)/shard_map/psum | solution.py:120
  62.1 15.9 %copy-start.2 = (f32[128,1,24]{2,1,0:T(1,128)}, f32[128,1,24]{2,1,0:T(1,128)S(1)}, u32[]{:S(2)}) copy-start(f32[128,1,24]{2,1,0:T(1,128)S(1)} %convert_element_type.31) | copy-start | bytes 36868
  117.8 12.4 %copy-start.4 = (f32[8]{0:T(128)S(1)}, f32[8]{0:T(128)}, u32[]{:S(2)}) copy-start(f32[8]{0:T(128)} %param.19) | copy-start | bytes 100
  130.2 119.2 %copy-start.3 = (s32[32,8]{0,1:T(8,128)S(1)}, s32[32,8]{0,1:T(8,128)}, u32[]{:S(2)}) copy-start(s32[32,8]{0,1:T(8,128)} %param.15) | copy-start | bytes 3076
  464.8 138.0 %copy-start.1 = (bf16[32,4096]{1,0:T(8,128)(2,1)S(1)}, bf16[32,4096]{1,0:T(8,128)(2,1)}, u32[]{:S(2)}) copy-start(bf16[32,4096]{1,0:T(8,128)(2,1)} %param.12) | copy-start | bytes 786436
  502.6 15.5 %all-to-all-start.3 = ((f32[128,1,24]{2,1,0:T(1,128)}), f32[128,1,24]{2,1,0:T(1,128)S(1)}, u32[]{:S(2)}, u32[]{:S(2)}) async-start(f32[128,1,24]{2,1,0:T(1,128)} %bitcast.22), calls=%async_computation.3 | async-start | bytes 131072 | tf_op jit(solution)/shard_map/all_to_all | solution.py:123
  509.2 91.5 %all-reduce.5.cloned.1.call-start = ((), (), s32[]{:S(2)}) async-start(), calls=%async_computation.5 | async-start | bytes 1048576 | tf_op jit(solution)/shard_map/psum | solution.py:120
Sparse Core Ops, SparseCore 0:
  249.5 81.8 all-reduce.2
  514.2 86.5 all-reduce.4
where the time goes:
time: 613 us; the launch traced here: 610 us
  waiting for transfers between devices  160 us (26%)
  matrix products  156 us (25%)
  local copies, waits for them, and re-layouts  81.5 us (13%)
  other arithmetic  79.3 us (13%)
  blocking collectives  75.2 us (12%)
  starting transfers between devices  33 us (5%)
  between operations  14.3 us (2%)
  loops' own time  10.3 us (2%)
    psum x2, waiting for transfers between devices, per_device(): sums, counts = lax.psum((sums, counts), 'post')  123 us
    dot_general x16, matrix products, expect(): jnp.dot(weighted.T, resid, precision=lax.Precision.HIGHEST, preferred_ele...  82.9 us
    psum x2, blocking collectives, per_device(): sums, counts = lax.psum((sums, counts), 'post')  75.2 us
    dot_general x16, matrix products, expect(): jnp.dot(resid, words.T, precision=lax.Precision.HIGHEST, preferred_elemen...  73.3 us
    reduce_sum x16, other arithmetic, expect(): jnp.sum(resid * resid, axis=1)[:, None] - 2.0 * cross  30.1 us
    all_to_all x1, waiting for transfers between devices, per_device(): lax.all_to_all(blocks.reshape(posting_count * n_sub, slot_capacity, dim_s...  24.1 us
    dynamic_slice x32, local copies, waits for them, and re-layouts, per_device(): sums, counts, errors = lax.map(one_sub, (resid, words, variance))  17.4 us
    gather x1, local copies, waits for them, and re-layouts, per_device(): nearest = centroids[ids]  15.7 us
  transfers between devices with their start and end apart: 6, of which 5 were waited for; matrix products, arithmetic and copies ran while one was open for 6% of the time, Pallas kernels for 0%

commit v1 on v0

v1 whole, which is shorter than its diff:
```python
import functools
import math

import jax
import jax.numpy as jnp
from jax import lax
from jax.experimental import pallas as pl
from jax.experimental.pallas import tpu as pltpu
from jax.sharding import Mesh
from jax.sharding import PartitionSpec as P

LOG2E = math.log2(math.e)
F32 = jnp.float32
BF16 = jnp.bfloat16
NT = (((1,), (1,)), ((), ()))
NN = (((1,), (0,)), ((), ()))
WINDOW = 64
TILE = 512
CAP = 768


def dot(a, b, dims=NN):
    return lax.dot_general(a, b, dims, preferred_element_type=F32)


def iota(shape, dim):
    return lax.broadcasted_iota(jnp.int32, shape, dim)


def ones_where(cond):
    return jnp.where(cond, 1.0, 0.0).astype(BF16)


def params(mib=48):
    return pltpu.CompilerParams(vmem_limit_bytes=mib << 20)


VMEM = pl.BlockSpec(memory_space=pltpu.VMEM)
SMEM = pl.BlockSpec(memory_space=pltpu.SMEM)


def block_place(r):
    d = lax.shift_right_logical(r, 1)
    y = lax.shift_right_logical(d, 3) & 3
    q = lax.shift_right_logical(d, 5) * 8 + (d & 7)
    return y, q


def list_kernel(cap, me_ref, ids_ref, out_ref):
    ids = ids_ref[...]
    mine = lax.shift_right_arithmetic(ids, 13) == me_ref[0]
    local = ids & 8191
    lane = iota((256, 128), 1)
    y, q = block_place(iota((256, 128), 0))
    keep = (q & 3) == lax.shift_right_logical(lane, 5)
    fold = ones_where((iota((128, 128), 0) & 31) == (iota((128, 128), 1) & 31))
    yc, qc = block_place(iota((32, 256), 1))
    pick = ones_where(yc * 8 + lax.shift_right_logical(qc, 2) == iota((32, 256), 0))

    def rows(x):
        x = dot(jnp.where(mine, x, 0).astype(F32).astype(BF16), fold)
        return dot(pick, jnp.where(keep, x, 0.0).astype(BF16))

    has = rows(jnp.ones_like(local))
    high = rows(lax.shift_right_logical(local, 7))
    low = rows(local & 127)
    has16 = has.astype(BF16)
    before = ones_where(iota((128, 128), 0) < iota((128, 128), 1))
    total = dot(has16, jnp.ones((128, 128), BF16))
    i0, i1 = iota((32, 32), 0), iota((32, 32), 1)
    earlier = ones_where((i1 < i0) & (lax.shift_right_logical(i1, 3) == lax.shift_right_logical(i0, 3)))
    rank = dot(has16, before) + dot(earlier, total.astype(BF16))
    rank = jnp.where(has > 0.5, rank, -1.0)
    sub = iota((8, 128), 0)
    place = iota((cap, 128), 0).astype(F32)
    for quarter in range(4):
        lhs, rhs = [], []
        for i in range(quarter * 8, quarter * 8 + 8):
            h = jnp.broadcast_to(high[i : i + 1], (8, 128))
            lo = jnp.broadcast_to(low[i : i + 1], (8, 128))
            lhs.append(jnp.where(sub == 0, h, jnp.where(sub == 1, lo, 0.0)).astype(BF16))
            rhs.append(ones_where(place == rank[i : i + 1]))
        got = dot(jnp.concatenate(lhs, 1), jnp.concatenate(rhs, 1), NT)
        out_ref[quarter : quarter + 1, :] = (got[0:1] * 128.0 + got[1:2]).astype(jnp.int32)


def key_kernel(cap, me_ref, ids_ref, key_ref, base_ref):
    owner = lax.shift_right_arithmetic(ids_ref[...], 13)
    lane = iota((256, 128), 1)
    count = jnp.zeros((256, 128), F32)
    for p in range(16):
        n = jnp.sum(jnp.where(owner == p, 1.0, 0.0), axis=1, keepdims=True)
        count = jnp.where(lane == p, n, count)
    count = count.astype(BF16)
    y, q = block_place(iota((32, 256), 1))
    b = iota((32, 256), 0)
    here = y == me_ref[0]
    start = dot(ones_where(here & (q < b)), count)
    first = dot(ones_where(here & (q < (b & ~1))), count).astype(jnp.int32)
    base = jnp.minimum(first & ~15, cap - WINDOW)
    base_ref[...] = base
    shift = (start - base.astype(F32)).astype(BF16)
    spread = ones_where(lax.shift_right_logical(iota((128, 1024), 1), 6) == iota((128, 1024), 0))
    gap = dot(shift, spread)
    col = iota((32, 1024), 1)
    key_ref[...] = jnp.where((col & 63).astype(F32) >= gap, col.astype(F32) - gap, -1.0)


def select_kernel(base_ref, key_ref, rows_ref, list_ref, out_ref):
    g = pl.program_id(0)
    parts = []
    for p in range(16):
        at = pl.multiple_of(base_ref[2 * g, p], 16)
        parts.append(list_ref[p, pl.ds(at, WINDOW), :])
    window = jnp.concatenate(parts, 0)
    meta = rows_ref[...].astype(F32)
    key = key_ref[0]
    hot = []
    for t in range(8):
        want = meta[:, t : t + 1] * 64.0 + meta[:, 8 + t : 9 + t]
        hot.append(ones_where(want[0:32] == key[0:1]))
        hot.append(ones_where(want[32:64] == key[1:2]))
    got = dot(jnp.concatenate(hot, 0), window).astype(BF16)
    for t in range(8):
        out_ref[t] = got[64 * t : 64 * t + 64]


def combine(parts, words):
    p0, p1, p2, p3 = parts
    total = (p0[...] + p2[...]) + (p1[...] + p3[...])

    def column(a):
        row = jnp.concatenate([total[256 + 2 * a : 257 + 2 * a], total[257 + 2 * a : 258 + 2 * a]], 1)
        return jnp.broadcast_to(row, (128, 256)).T

    count = jnp.where(iota((256, 128), 1) < 64, column(0), column(1))
    return (total[0:256] + words) / (count + 1.0)


def em_kernel(last, *refs):
    if last:
        p0, p1, p2, p3, rows_ref, cent_ref, words_ref, var_ref, out_ref, new_ref, err_ref = refs[:11]
        words = combine((p0, p1, p2, p3), words_ref[...])
        new_ref[...] = words
    else:
        rows_ref, cent_ref, words_ref, var_ref, out_ref = refs[:5]
        words = words_ref[...]
    mat_ref, weight_ref, acc_ref, count_ref = refs[-4:]
    scale = LOG2E / var_ref[...]
    scaled = words * scale
    left = iota((256, 128), 1) < 64
    biases = []
    for a in range(2):
        on = left if a == 0 else jnp.logical_not(left)
        x = jnp.where(on, scaled, 0.0)
        hi = x.astype(BF16).astype(F32)
        lo = x - hi
        mat_ref[a, :, 0:128] = hi.astype(BF16)
        mat_ref[a, :, 128:256] = (-hi).astype(BF16)
        mat_ref[a, :, 256:384] = lo.astype(BF16)
        mat_ref[a, :, 384:512] = (-lo).astype(BF16)
        biases.append(0.5 * jnp.sum(x * words, axis=1, keepdims=True))
    for c in range(8):
        flipped = rows_ref[128 * c : 128 * c + 128, 128:256].astype(F32).T
        weight_ref[:, 128 * c : 128 * c + 128] = flipped[16:24]
    acc_ref[...] = jnp.zeros_like(acc_ref)
    count_ref[...] = jnp.zeros_like(count_ref)

    def slots(t, carry):
        for c in range(1024 // TILE):
            at = pl.ds(c * TILE, TILE)
            v = rows_ref[at, 0:128]
            cent = cent_ref[t, at, :]
            x = jnp.concatenate([v, cent], 1)
            xx = jnp.concatenate([x, x], 1)
            tall = jnp.concatenate([x, x], 0)
            weight = weight_ref[pl.ds(t, 1), at]
            if last:
                r = v.astype(F32) - cent.astype(F32)
                r2 = r * r
                hi = r2.astype(BF16)
                lo = (r2 - hi.astype(F32)).astype(BF16)
                error = dot(jnp.ones((8, 256), BF16), jnp.concatenate([hi, lo], 1), NT)[0:1]
            for a in range(2):
                s = dot(mat_ref[a], xx, NT) - biases[a]
                top = jnp.max(s, axis=0, keepdims=True)
                e = jnp.exp2(s - top)
                inv = 1.0 / jnp.sum(e, axis=0, keepdims=True)
                if last:
                    mean = jnp.sum(e * s, axis=0, keepdims=True) * inv
                    error = error - mean * (2.0 / scale[0:1, 64 * a : 64 * a + 1])
                w = e * (inv * weight)
                w_hi = w.astype(BF16)
                w_lo = (w - w_hi.astype(F32)).astype(BF16)
                acc_ref[a] += dot(jnp.concatenate([w_hi, w_lo], 1), tall)
                n = w[:, 0:128]
                for k in range(1, TILE // 128):
                    n = n + w[:, 128 * k : 128 * k + 128]
                count_ref[a] += n
            if last:
                err_ref[pl.ds(t, 1), at] = error
        return carry

    lax.fori_loop(0, 8, slots, 0)
    diff = [acc_ref[a, :, 0:128] - acc_ref[a, :, 128:256] for a in range(2)]
    out_ref[0:256] = jnp.where(left, diff[0], diff[1])
    tail = []
    for a in range(2):
        row = jnp.sum(count_ref[a].T, axis=0, keepdims=True)
        tail += [row[:, 0:128], row[:, 128:256]]
    tail.append(jnp.zeros((4, 128), F32))
    out_ref[256:264] = jnp.concatenate(tail, 0)


def em(last, args):
    shapes = [jax.ShapeDtypeStruct((264, 128), F32)]
    if last:
        shapes += [jax.ShapeDtypeStruct((256, 128), F32), jax.ShapeDtypeStruct((8, 1024), F32)]
    return pl.pallas_call(
        functools.partial(em_kernel, last),
        out_shape=shapes,
        in_specs=[VMEM] * len(args),
        out_specs=[VMEM] * len(shapes),
        scratch_shapes=[
            pltpu.VMEM((2, 256, 512), BF16),
            pltpu.VMEM((8, 1024), F32),
            pltpu.VMEM((2, 256, 256), F32),
            pltpu.VMEM((2, 256, 128), F32),
        ],
        compiler_params=params(),
        name="em_last" if last else "em_first",
    )(*args)


def update_kernel(p0, p1, p2, p3, words_ref, out_ref):
    out_ref[...] = combine((p0, p1, p2, p3), words_ref[...])


def assemble_kernel(z_ref, x0, x1, x2, x3, out_ref):
    for d, x in enumerate((x0, x1, x2, x3)):
        at = 2 * ((z_ref[0] + (4 - d)) & 3)
        out_ref[at] = x[:, 0:64]
        out_ref[at + 1] = x[:, 64:128]


def shifts(x, axis):
    return [x] + [lax.ppermute(x, axis, [(i, (i + d) % 4) for i in range(4)]) for d in (1, 2, 3)]


def per_device(vectors, owner, local, mask, slot_weight, centroids, codebook, variance):
    z, y = lax.axis_index("z"), lax.axis_index("y")
    me = (z * 4 + y).astype(jnp.int32).reshape(1)
    y1, z1 = y.astype(jnp.int32).reshape(1), z.astype(jnp.int32).reshape(1)
    valid = mask > 0
    owned = jnp.where(valid, owner, -1)

    posting = jnp.where(valid, owner * 8192 + local, -1).T.reshape(1, 2, 128)
    ids = lax.all_to_all(
        jnp.broadcast_to(posting, (128, 2, 128)), ("z", "y", "sub"), 0, 0, tiled=True
    ).reshape(256, 128)

    wanted = pl.pallas_call(
        functools.partial(list_kernel, CAP),
        out_shape=jax.ShapeDtypeStruct((4, CAP), jnp.int32),
        in_specs=[SMEM, VMEM],
        out_specs=VMEM,
        compiler_params=params(),
        name="lists",
    )(me, ids)
    found = centroids.at[wanted.reshape(4 * CAP)].get(mode="promise_in_bounds")
    found = found.reshape(4, CAP, 4, 128).transpose(2, 0, 1, 3).reshape(16, CAP, 128)
    lists = lax.all_to_all(found, ("z", "y"), 0, 0, tiled=True)

    names = jnp.any(owned[:, :, None] == jnp.arange(16)[None, None, :], axis=1)
    upto = jnp.dot(jnp.tril(jnp.ones((32, 32), F32), -1), names.astype(F32))
    rank = jnp.sum(jnp.where(owned[:, :, None] == jnp.arange(16)[None, None, :], upto[:, None, :], 0.0), axis=2)
    weight = slot_weight * mask.astype(slot_weight.dtype)
    meta = jnp.concatenate([owned.astype(BF16), rank.astype(BF16), weight, jnp.zeros((32, 104), BF16)], 1)
    packed = jnp.concatenate(
        [
            vectors.reshape(32, 8, 4, 128).transpose(2, 1, 0, 3).reshape(32, 32, 128),
            jnp.broadcast_to(meta, (32, 32, 128)),
        ],
        2,
    )
    rows = lax.all_to_all(packed, ("z", "sub"), 0, 0, tiled=True).reshape(1024, 256)

    keys, base = pl.pallas_call(
        functools.partial(key_kernel, CAP),
        out_shape=(jax.ShapeDtypeStruct((32, 1024), F32), jax.ShapeDtypeStruct((32, 128), jnp.int32)),
        in_specs=[SMEM, VMEM],
        out_specs=(VMEM, VMEM),
        compiler_params=params(),
        name="keys",
    )(y1, ids)

    cents = pl.pallas_call(
        select_kernel,
        out_shape=jax.ShapeDtypeStruct((8, 1024, 128), BF16),
        grid_spec=pltpu.PrefetchScalarGridSpec(
            num_scalar_prefetch=1,
            grid=(16,),
            in_specs=[
                pl.BlockSpec((1, 2, 1024), lambda g, b: (g, 0, 0)),
                pl.BlockSpec((64, 128), lambda g, b: (g, 1)),
                pl.BlockSpec((16, CAP, 128), lambda g, b: (0, 0, 0)),
            ],
            out_specs=pl.BlockSpec((8, 64, 128), lambda g, b: (0, g, 0)),
        ),
        compiler_params=params(),
        name="select",
    )(base, keys.reshape(16, 2, 1024), rows, lists)

    words = lax.dynamic_slice(codebook, (2 * z, 0, 0), (2, 256, 64)).transpose(1, 0, 2).reshape(256, 128)
    spread = jnp.repeat(lax.dynamic_slice(variance, (2 * z,), (2,)), 64).reshape(1, 128)
    (part,) = em(False, (rows, cents, words, spread))
    part, words, error = em(True, (*shifts(part, "y"), rows, cents, words, spread))
    words = pl.pallas_call(
        update_kernel,
        out_shape=jax.ShapeDtypeStruct((256, 128), F32),
        in_specs=[VMEM] * 5,
        out_specs=VMEM,
        name="update",
    )(*shifts(part, "y"), words)
    trained = pl.pallas_call(
        assemble_kernel,
        out_shape=jax.ShapeDtypeStruct((8, 256, 64), F32),
        in_specs=[SMEM] + [VMEM] * 4,
        out_specs=VMEM,
        name="assemble",
    )(z1, *shifts(words, "z"))

    error = error.reshape(8, 32, 32).transpose(1, 0, 2)
    error = jnp.sum(lax.all_to_all(error, ("z", "sub"), 0, 0, tiled=True), axis=0).T
    return trained, error / vectors.shape[1] * mask.astype(F32)


def solution(mesh):
    grid = Mesh(mesh.devices.reshape(4, 4, 8), ("z", "y", "sub"))
    rows = P(("z", "y", "sub"), None)
    return jax.shard_map(
        per_device,
        mesh=grid,
        in_specs=(rows, rows, rows, rows, rows, P(("z", "y"), "sub"), P("sub", None, None), P("sub")),
        out_specs=(P("sub", None, None), rows),
        check_vma=False,
    )
```

time: 613 us -> 204 us (0.33)
  matrix products: 156 us -> 0.19 us
  waiting for transfers between devices: 160 us -> 58.8 us
  other arithmetic: 79.3 us -> 4.57 us
  blocking collectives: 75.2 us -> 13.1 us
  Pallas kernels: 0 us -> 52.6 us
  local copies, waits for them, and re-layouts: 81.5 us -> 35.6 us
  between operations: 14.3 us -> 0.91 us
  loops' own time: 10.3 us -> 0 us
    dot_general x32 -> x1, matrix products: 156 us -> 0.19 us  [per_device(): upto = jnp.dot(jnp.tril(jnp.ones((32, 32), F32), -1), names.astype(F32))]
    psum x2 -> x0, waiting for transfers between devices: 123 us -> none  [per_device(): sums, counts = lax.psum((sums, counts), 'post')]
    psum x2 -> x0, blocking collectives: 75.2 us -> none  [per_device(): sums, counts = lax.psum((sums, counts), 'post')]
    reduce_sum x67 -> x2, other arithmetic: 62.9 us -> 0.07 us  [the longest x1 0.04 us: per_device(): jnp.sum(lax.all_to_all(error, ('z', 'sub'), 0, 0, tiled=True), axis=0)]
    pallas_call x0 -> x7, Pallas kernels: none -> 52.6 us  [the longest x2 33 us: em(): pl.pallas_call(functools.partial(em_kernel, last), out_shape=shapes, in_s...]
    dynamic_slice x32 -> x2, local copies, waits for them, and re-layouts: 17.4 us -> 0.1 us  [the longest x1 0.08 us: per_device(): lax.dynamic_slice(variance, (2 * z,), (2,))]
    ppermute x0 -> x9, starting transfers between devices: none -> 16.1 us  [shifts(): lax.ppermute(x, axis, [(i, (i + d) % 4) for i in range(4)])]
    all_to_all x0 -> x1, blocking collectives: none -> 13.1 us  [per_device(): lax.all_to_all(error, ('z', 'sub'), 0, 0, tiled=True)]
  transfers between devices with their start and end apart: 6 -> 12, of which waited for: 5 -> 7; matrix products, arithmetic and copies ran while one was open for 6% -> 17% of each run, Pallas kernels for 0% -> 2%
where the time goes in v1:
time: 204 us; the launch traced here: 203 us
  waiting for transfers between devices  58.8 us (29%)
  Pallas kernels  52.6 us (26%)
  starting transfers between devices  37.4 us (18%)
  local copies, waits for them, and re-layouts  35.6 us (17%)
  blocking collectives  13.1 us (6%)
  other arithmetic  4.57 us (2%)
    all_to_all x1, waiting for transfers between devices, per_device(): lists = lax.all_to_all(found, ('z', 'y'), 0, 0, tiled=True)  42.9 us
    pallas_call x2, Pallas kernels, em(): pl.pallas_call(functools.partial(em_kernel, last), out_shape=shapes, in_s...  33 us
    gather x1, local copies, waits for them, and re-layouts, per_device(): found = centroids.at[wanted.reshape(4 * CAP)].get(mode='promise_in_bounds')  17.9 us
    ppermute x9, starting transfers between devices, shifts(): lax.ppermute(x, axis, [(i, (i + d) % 4) for i in range(4)])  16.1 us
    all_to_all x1, blocking collectives, per_device(): lax.all_to_all(error, ('z', 'sub'), 0, 0, tiled=True)  13.1 us
    pallas_call x1, Pallas kernels, per_device(): pl.pallas_call(select_kernel, out_shape=jax.ShapeDtypeStruct((8, 1024, 12...  12.1 us
    ppermute x9, waiting for transfers between devices, shifts(): lax.ppermute(x, axis, [(i, (i + d) % 4) for i in range(4)])  11.2 us
    all_to_all x1, starting transfers between devices, per_device(): lax.all_to_all(jnp.broadcast_to(posting, (128, 2, 128)), ('z', 'y', 'sub'...  10.4 us
  transfers between devices with their start and end apart: 12, of which 7 were waited for; matrix products, arithmetic and copies ran while one was open for 17% of the time, Pallas kernels for 2%

profile of v1, /device:TPU:8, one launch (start us, length us, event | category | flops | bytes accessed | tf_op | source)
XLA Modules:
  0.0 203.2 jit_solution(10558889101101538814)
XLA Ops:
  0.6 0.8 select_bitcast_fusion
  1.5 0.7 broadcast_in_dim.54
  2.2 10.4 %all-to-all-start.1 = ((s32[128,2,128]{2,1,0:T(2,128)}), s32[128,2,128]{2,1,0:T(2,128)S(1)}, u32[]{:S(2)}, u32[]{:S(2)}) async-start(s32[128,2,128]{2,1,0:T(2,128)} %broadcast_in_dim.54), calls=%async_computation.1 | async-start | bytes 262144 | tf_op jit(solution)/shard_map/all_to_all | solution.py:258
  12.7 0.7 fusion.8
  13.4 0.2 fusion.1
  13.8 0.7 convert_multiply_fusion
  14.5 0.1 copy.40
  14.8 1.1 reshape.76
  15.9 0.1 copy.37
  16.1 0.9 pad_maximum_fusion
  16.9 4.8 %all-to-all-done.1 = s32[128,2,128]{2,1,0:T(2,128)S(1)} async-done(((s32[128,2,128]{2,1,0:T(2,128)}), s32[128,2,128]{2,1,0:T(2,128)S(1)}, u32[]{:S(2)}, u32[]{:S(2)}) %all-to-all-start.1) | async-done | bytes 131104 | tf_op jit(solution)/shard_map/all_to_all | solution.py:258
  21.7 3.9 %all-to-all-start = ((bf16[32,32,256]{2,1,0:T(8,128)(2,1)}), bf16[32,32,256]{2,1,0:T(8,128)(2,1)S(1)}, u32[]{:S(2)}, u32[]{:S(2)}) async-start(bf16[32,32,256]{2,1,0:T(8,128)(2,1)} %pad_maximum_fusion), calls=%async_computation | async-start | bytes 1048576 | tf_op jit(solution)/shard_map/all_to_all | solution.py:286
  25.6 2.4 %lists.1 = s32[4,768]{1,0:T(4,128)S(1)} custom-call(s32[1]{0:T(128)} %bitcast.7.me_ref, s32[256,128]{1,0:T(8,128)S(1)} %bitcast.29), custom_call_target="tpu_custom_call" | custom-call | tf_op jit(solution)/shard_map/lists/pallas_call | solution.py:262
  28.1 17.9 %gather_fusion = bf16[3072,512]{1,0:T(8,128)(2,1)} fusion(bf16[8192,512]{1,0:T(8,128)(2,1)} %param.13, s32[3072]{0:T(1024)S(1)} %broadcast_clamp_fusion), kind=kCustom, calls=%fused_computation | custom fusion | bytes 6303744 | tf_op jit(solution)/shard_map/gather | solution.py:270
  45.9 5.5 %reshape.84 = bf16[4,768,4,128]{3,2,1,0:T(4,128)(2,1)} reshape(bf16[3072,512]{1,0:T(8,128)(2,1)} %gather_fusion) | data formatting | bytes 6291456 | tf_op jit(solution)/shard_map/reshape | solution.py:271
  51.4 4.2 %copy.41 = bf16[4,768,4,128]{3,1,0,2:T(8,128)(2,1)} copy(bf16[4,768,4,128]{3,2,1,0:T(4,128)(2,1)} %reshape.84) | data formatting | bytes 6291456 | tf_op jit(solution)/shard_map/reshape | solution.py:271
  55.6 6.9 %all-to-all-start.2 = ((bf16[16,768,128]{2,1,0:T(8,128)(2,1)}), bf16[16,768,128]{2,1,0:T(8,128)(2,1)}, u32[]{:S(2)}, u32[]{:S(2)}) async-start(bf16[16,768,128]{2,1,0:T(8,128)(2,1)} %bitcast.32), calls=%async_computation.2 | async-start | bytes 6291456 | tf_op jit(solution)/shard_map/all_to_all | solution.py:272
  62.9 0.9 keys.1
  63.8 42.9 %all-to-all-done.2.list_ref = bf16[16,768,128]{2,1,0:T(8,128)(2,1)} async-done(((bf16[16,768,128]{2,1,0:T(8,128)(2,1)}), bf16[16,768,128]{2,1,0:T(8,128)(2,1)}, u32[]{:S(2)}, u32[]{:S(2)}) %all-to-all-start.2) | async-done | bytes 3145760 | tf_op jit(solution)/shard_map/all_to_all | solution.py:272
  106.7 12.1 %select.1.refs_1_.refs_5_ = bf16[8,1024,128]{2,1,0:T(8,128)(2,1)S(1)} custom-call(s32[32,128]{1,0:T(8,128)S(1)} %get-tuple-element.7.base_ref, f32[16,2,1024]{2,1,0:T(2,128)S(1)} %reshape.81.key_ref, bf16[1024,256]{1,0:T(8,128)(2,1)S(1)} %bitcast.26, bf16[16,768,128]{2,1,0:T(8,128)(2,1)} %all-to-all-done.2.list_ref), custom_call_target="tpu_custom_call" | custom-call | tf_op jit(solution)/shard_map/select/pallas_call | solution.py:297
  118.9 14.4 %em_first.1.refs_0_ = f32[264,128]{1,0:T(8,128)S(1)} custom-call(bf16[1024,256]{1,0:T(8,128)(2,1)S(1)} %bitcast.27, bf16[8,1024,128]{2,1,0:T(8,128)(2,1)S(1)} %select.1.refs_1_.refs_5_, f32[256,128]{1,0:T(8,128)S(1)} %copy.42.refs_2_.refs_6_, f32[1,128]{1,0:T(1,128)S(1)} %reshape_reshape.3.refs_3_.refs_7_), custom_call_target="tpu_custom_call" | custom-call | tf_op jit(solution)/shard_map/em_first/pallas_call | solution.py:219
  133.3 0.8 collective-permute-start
  134.2 5.7 %collective-permute-start.1 = (f32[264,128]{1,0:T(8,128)S(1)}, f32[264,128]{1,0:T(8,128)S(1)}, u32[]{:S(2)}, u32[]{:S(2)}) collective-permute-start(f32[264,128]{1,0:T(8,128)S(1)} %em_first.1.refs_0_), channel_id=1, source_target_pairs={{0,16},{8,24},{16,0},{24,8},{1,17},{9,25},{17,1},{25,9},{2,18},{10... | collective-permute-start | bytes 405512 | tf_op jit(solution)/shard_map/ppermute | solution.py:247
  139.9 0.1 collective-permute-start.2
  140.0 2.2 %collective-permute-done.refs_1_ = f32[264,128]{1,0:T(8,128)S(1)} collective-permute-done((f32[264,128]{1,0:T(8,128)S(1)}, f32[264,128]{1,0:T(8,128)S(1)}, u32[]{:S(2)}, u32[]{:S(2)}) %collective-permute-start) | collective-permute-done | bytes 135200 | tf_op jit(solution)/shard_map/ppermute | solution.py:247
  142.3 1.6 collective-permute-done.1.refs_2_
  143.9 1.4 collective-permute-done.2.refs_3_
  145.3 18.6 %em_last.1 = (f32[264,128]{1,0:T(8,128)S(1)}, f32[256,128]{1,0:T(8,128)S(1)}, f32[8,1024]{1,0:T(8,128)S(1)}) custom-call(f32[264,128]{1,0:T(8,128)S(1)} %em_first.1.refs_0_, f32[264,128]{1,0:T(8,128)S(1)} %collective-permute-done.refs_1_, f32[264,128]{1,0:T(8,128)S(1)} %collective-permute-done.1.refs_2_, f32[264,128]{1,0:T(8,128)S(1)} %collective-permute-done.2.refs_3_, ...), custom_call_target="tpu_custom_call" | custom-call | tf_op jit(solution)/shard_map/em_last/pallas_call | solution.py:219
  163.9 0.6 copy-done.2
  164.5 0.5 collective-permute-start.3
  165.1 3.3 %collective-permute-start.4 = (f32[264,128]{1,0:T(8,128)S(1)}, f32[264,128]{1,0:T(8,128)S(1)}, u32[]{:S(2)}, u32[]{:S(2)}) collective-permute-start(f32[264,128]{1,0:T(8,128)S(1)} %get-tuple-element.9.p0), channel_id=1, source_target_pairs={{0,16},{8,24},{16,0},{24,8},{1,17},{9,25},{17,1},{25,9},{2,18},{10... | collective-permute-start | bytes 405512 | tf_op jit(solution)/shard_map/ppermute | solution.py:247
  168.4 1.7 collective-permute-start.5
  170.1 0.1 reshape.87
  170.3 0.1 reshape.96
  170.4 13.1 %all_to_all.20 = f32[32,1,256]{2,1,0:T(1,128)S(1)} all-to-all(f32[32,1,256]{2,1,0:T(1,128)S(1)} %reshape.96), channel_id=1, replica_groups=mesh['z'=4,'y'=4,'sub'=8] {'z','sub'}, dimensions={0} | all-to-all | bytes 65536 | tf_op jit(solution)/shard_map/all_to_all | solution.py:334
  183.5 0.5 broadcast.27
  184.0 0.7 reduce
  184.9 0.6 copy-done.3
  185.6 2.0 update.1.x0
  187.6 0.6 collective-permute-start.6
  188.2 2.0 collective-permute-start.7
  190.2 1.2 collective-permute-start.8
  191.5 0.6 bitcast_multiply_fusion
  192.1 5.3 %collective-permute-done.6.x1 = f32[256,128]{1,0:T(8,128)S(1)} collective-permute-done((f32[256,128]{1,0:T(8,128)}, f32[256,128]{1,0:T(8,128)S(1)}, u32[]{:S(2)}, u32[]{:S(2)}) %collective-permute-start.6) | collective-permute-done | bytes 131104 | tf_op jit(solution)/shard_map/ppermute | solution.py:247
  197.3 0.6 collective-permute-done.8.x3
  198.0 0.6 copy-done.8
  198.6 2.3 %assemble.1 = f32[8,256,64]{2,1,0:T(8,128)} custom-call(s32[1]{0:T(128)} %bitcast.z_ref, f32[256,128]{1,0:T(8,128)} %update.1.x0, f32[256,128]{1,0:T(8,128)} %copy-done.6, f32[256,128]{1,0:T(8,128)} %copy-done.7, f32[256,128]{1,0:T(8,128)} %copy-done.8), custom_call_target="tpu_custom_call" | custom-call | tf_op jit(solution)/shard_map/assemble/pallas_call | solution.py:325
  200.9 2.3 %copy.45 = f32[8,256,64]{1,2,0:T(8,128)} copy(f32[8,256,64]{2,1,0:T(8,128)} %assemble.1) | data formatting | bytes 1048576
  (46 shorter events, 1.4 us)
Async XLA Ops:
  0.6 61.9 %copy-start = (f32[8,256,64]{1,2,0:T(8,128)S(1)}, f32[8,256,64]{1,2,0:T(8,128)}, u32[]{:S(2)}) copy-start(f32[8,256,64]{1,2,0:T(8,128)} %param.14) | copy-start | bytes 1572868
  2.2 19.5 %all-to-all-start.1 = ((s32[128,2,128]{2,1,0:T(2,128)}), s32[128,2,128]{2,1,0:T(2,128)S(1)}, u32[]{:S(2)}, u32[]{:S(2)}) async-start(s32[128,2,128]{2,1,0:T(2,128)} %broadcast_in_dim.54), calls=%async_computation.1 | async-start | bytes 262144 | tf_op jit(solution)/shard_map/all_to_all | solution.py:258
  21.7 33.9 %all-to-all-start = ((bf16[32,32,256]{2,1,0:T(8,128)(2,1)}), bf16[32,32,256]{2,1,0:T(8,128)(2,1)S(1)}, u32[]{:S(2)}, u32[]{:S(2)}) async-start(bf16[32,32,256]{2,1,0:T(8,128)(2,1)} %pad_maximum_fusion), calls=%async_computation | async-start | bytes 1048576 | tf_op jit(solution)/shard_map/all_to_all | solution.py:286
  55.6 7.0 %copy-start.10 = (f32[8]{0:T(128)S(1)}, f32[8]{0:T(128)}, u32[]{:S(2)}) copy-start(f32[8]{0:T(128)} %param.15) | copy-start | bytes 100
  55.6 51.1 %all-to-all-start.2 = ((bf16[16,768,128]{2,1,0:T(8,128)(2,1)}), bf16[16,768,128]{2,1,0:T(8,128)(2,1)}, u32[]{:S(2)}, u32[]{:S(2)}) async-start(bf16[16,768,128]{2,1,0:T(8,128)(2,1)} %bitcast.32), calls=%async_computation.2 | async-start | bytes 6291456 | tf_op jit(solution)/shard_map/all_to_all | solution.py:272
  133.3 58.1 %copy-start.9 = (s32[32,8]{0,1:T(8,128)S(1)}, s32[32,8]{0,1:T(8,128)}, u32[]{:S(2)}) copy-start(s32[32,8]{0,1:T(8,128)} %param.11) | copy-start | bytes 3076
  133.3 8.9 %collective-permute-start = (f32[264,128]{1,0:T(8,128)S(1)}, f32[264,128]{1,0:T(8,128)S(1)}, u32[]{:S(2)}, u32[]{:S(2)}) collective-permute-start(f32[264,128]{1,0:T(8,128)S(1)} %em_first.1.refs_0_), channel_id=1, source_target_pairs={{0,8},{8,16},{16,24},{24,0},{1,9},{9,17},{17,25},{25,1},{2,10},{10... | collective-permute-start | bytes 405512 | tf_op jit(solution)/shard_map/ppermute | solution.py:247
  134.2 9.7 %collective-permute-start.1 = (f32[264,128]{1,0:T(8,128)S(1)}, f32[264,128]{1,0:T(8,128)S(1)}, u32[]{:S(2)}, u32[]{:S(2)}) collective-permute-start(f32[264,128]{1,0:T(8,128)S(1)} %em_first.1.refs_0_), channel_id=1, source_target_pairs={{0,16},{8,24},{16,0},{24,8},{1,17},{9,25},{17,1},{25,9},{2,18},{10... | collective-permute-start | bytes 405512 | tf_op jit(solution)/shard_map/ppermute | solution.py:247
  139.9 5.4 %collective-permute-start.2 = (f32[264,128]{1,0:T(8,128)S(1)}, f32[264,128]{1,0:T(8,128)S(1)}, u32[]{:S(2)}, u32[]{:S(2)}) collective-permute-start(f32[264,128]{1,0:T(8,128)S(1)} %em_first.1.refs_0_), channel_id=1, source_target_pairs={{0,24},{8,0},{16,8},{24,16},{1,25},{9,1},{17,9},{25,17},{2,26},{10... | collective-permute-start | bytes 405512 | tf_op jit(solution)/shard_map/ppermute | solution.py:247
  163.9 0.6 copy-start.2
  164.5 20.4 %copy-start.1 = (f32[264,128]{1,0:T(8,128)}, f32[264,128]{1,0:T(8,128)S(1)}, u32[]{:S(2)}) copy-start(f32[264,128]{1,0:T(8,128)S(1)} %get-tuple-element.9.p0) | copy-start | bytes 405508
  164.5 20.3 %collective-permute-start.3 = (f32[264,128]{1,0:T(8,128)S(1)}, f32[264,128]{1,0:T(8,128)S(1)}, u32[]{:S(2)}, u32[]{:S(2)}) collective-permute-start(f32[264,128]{1,0:T(8,128)S(1)} %get-tuple-element.9.p0), channel_id=1, source_target_pairs={{0,8},{8,16},{16,24},{24,0},{1,9},{9,17},{17,25},{25,1},{2,10},{10... | collective-permute-start | bytes 405512 | tf_op jit(solution)/shard_map/ppermute | solution.py:247
  165.1 19.8 %collective-permute-start.4 = (f32[264,128]{1,0:T(8,128)S(1)}, f32[264,128]{1,0:T(8,128)S(1)}, u32[]{:S(2)}, u32[]{:S(2)}) collective-permute-start(f32[264,128]{1,0:T(8,128)S(1)} %get-tuple-element.9.p0), channel_id=1, source_target_pairs={{0,16},{8,24},{16,0},{24,8},{1,17},{9,25},{17,1},{25,9},{2,18},{10... | collective-permute-start | bytes 405512 | tf_op jit(solution)/shard_map/ppermute | solution.py:247
  168.4 16.5 %collective-permute-start.5 = (f32[264,128]{1,0:T(8,128)S(1)}, f32[264,128]{1,0:T(8,128)S(1)}, u32[]{:S(2)}, u32[]{:S(2)}) collective-permute-start(f32[264,128]{1,0:T(8,128)S(1)} %get-tuple-element.9.p0), channel_id=1, source_target_pairs={{0,24},{8,0},{16,8},{24,16},{1,25},{9,1},{17,9},{25,17},{2,26},{10... | collective-permute-start | bytes 405512 | tf_op jit(solution)/shard_map/ppermute | solution.py:247
  184.8 0.7 copy-start.3
  184.9 0.7 copy-start.4
  184.9 0.7 copy-start.5
  187.6 9.7 %collective-permute-start.6 = (f32[256,128]{1,0:T(8,128)}, f32[256,128]{1,0:T(8,128)S(1)}, u32[]{:S(2)}, u32[]{:S(2)}) collective-permute-start(f32[256,128]{1,0:T(8,128)} %update.1.x0), channel_id=1, source_target_pairs={{0,32},{32,64},{64,96},{96,0},{1,33},{33,65},{65,97},{97,1},{2,34}... | collective-permute-start | bytes 393224 | tf_op jit(solution)/shard_map/ppermute | solution.py:247
  188.2 9.1 %collective-permute-start.7 = (f32[256,128]{1,0:T(8,128)}, f32[256,128]{1,0:T(8,128)S(1)}, u32[]{:S(2)}, u32[]{:S(2)}) collective-permute-start(f32[256,128]{1,0:T(8,128)} %update.1.x0), channel_id=1, source_target_pairs={{0,64},{32,96},{64,0},{96,32},{1,65},{33,97},{65,1},{97,33},{2,66}... | collective-permute-start | bytes 393224 | tf_op jit(solution)/shard_map/ppermute | solution.py:247
  190.2 7.7 %collective-permute-start.8 = (f32[256,128]{1,0:T(8,128)}, f32[256,128]{1,0:T(8,128)S(1)}, u32[]{:S(2)}, u32[]{:S(2)}) collective-permute-start(f32[256,128]{1,0:T(8,128)} %update.1.x0), channel_id=1, source_target_pairs={{0,96},{32,0},{64,32},{96,64},{1,97},{33,1},{65,33},{97,65},{2,98}... | collective-permute-start | bytes 393224 | tf_op jit(solution)/shard_map/ppermute | solution.py:247
  197.3 0.7 copy-start.6
  197.3 0.7 copy-start.7
  197.9 0.7 copy-start.8

commit v2 on v1

v2 whole, which is shorter than its diff:
```python
import functools
import math

import jax
import jax.numpy as jnp
from jax import lax
from jax.experimental import pallas as pl
from jax.experimental.pallas import tpu as pltpu
from jax.sharding import Mesh
from jax.sharding import PartitionSpec as P

LOG2E = math.log2(math.e)
F32 = jnp.float32
BF16 = jnp.bfloat16
NT = (((1,), (1,)), ((), ()))
NN = (((1,), (0,)), ((), ()))
WINDOW = 64
TILE = 512
CAP = 384


def dot(a, b, dims=NN):
    return lax.dot_general(a, b, dims, preferred_element_type=F32)


def iota(shape, dim):
    return lax.broadcasted_iota(jnp.int32, shape, dim)


def ones_where(cond):
    return jnp.where(cond, 1.0, 0.0).astype(BF16)


def params(mib=48):
    return pltpu.CompilerParams(vmem_limit_bytes=mib << 20)


VMEM = pl.BlockSpec(memory_space=pltpu.VMEM)
SMEM = pl.BlockSpec(memory_space=pltpu.SMEM)


def block_place(r):
    d = lax.shift_right_logical(r, 1)
    y = lax.shift_right_logical(d, 3) & 3
    q = lax.shift_right_logical(d, 5) * 8 + (d & 7)
    return y, q


def list_kernel(me_ref, ids_ref, first_ref, second_ref):
    ids = ids_ref[...]
    mine = lax.shift_right_arithmetic(ids, 13) == me_ref[0]
    local = ids & 8191
    lane = iota((256, 128), 1)
    _, q = block_place(iota((256, 128), 0))
    keep = (q & 3) == lax.shift_right_logical(lane, 5)
    fold = ones_where((iota((128, 128), 0) & 31) == (iota((128, 128), 1) & 31))
    yc, qc = block_place(iota((32, 256), 1))
    pick = ones_where(yc * 8 + lax.shift_right_logical(qc, 2) == iota((32, 256), 0))

    def rows(x):
        x = dot(jnp.where(mine, x, 0).astype(F32).astype(BF16), fold)
        return dot(pick, jnp.where(keep, x, 0.0).astype(BF16))

    has = rows(jnp.ones_like(local))
    high = rows(lax.shift_right_logical(local, 7))
    low = rows(local & 127)
    has16 = has.astype(BF16)
    before = ones_where(iota((128, 128), 0) < iota((128, 128), 1))
    total = dot(has16, jnp.ones((128, 128), BF16))
    i0, i1 = iota((32, 32), 0), iota((32, 32), 1)
    earlier = ones_where((i1 < i0) & (lax.shift_right_logical(i1, 2) == lax.shift_right_logical(i0, 2)))
    rank = dot(has16, before) + dot(earlier, total.astype(BF16))
    rank = jnp.where(has > 0.5, rank, -1.0)
    sub = iota((8, 128), 0)
    place = iota((CAP, 128), 0).astype(F32)
    for group in range(8):
        lhs, rhs = [], []
        for i in range(group * 4, group * 4 + 4):
            h = jnp.broadcast_to(high[i : i + 1], (8, 128))
            lo = jnp.broadcast_to(low[i : i + 1], (8, 128))
            lhs.append(jnp.where(sub == 0, h, jnp.where(sub == 1, lo, 0.0)).astype(BF16))
            rhs.append(ones_where(place == rank[i : i + 1]))
        got = dot(jnp.concatenate(lhs, 1), jnp.concatenate(rhs, 1), NT)
        out_ref = (first_ref, second_ref)[group % 2]
        quarter = group // 2
        out_ref[quarter : quarter + 1, :] = (got[0:1] * 128.0 + got[1:2]).astype(jnp.int32)


def key_kernel(me_ref, ids_ref, key_ref, base_ref):
    owner = lax.shift_right_arithmetic(ids_ref[...], 13)
    lane = iota((256, 128), 1)
    count = jnp.zeros((256, 128), F32)
    for p in range(16):
        n = jnp.sum(jnp.where(owner == p, 1.0, 0.0), axis=1, keepdims=True)
        count = jnp.where(lane == p, n, count)
    count = count.astype(BF16)
    y, q = block_place(iota((32, 256), 1))
    b = iota((32, 256), 0)
    here = (y == me_ref[0]) & (lax.shift_right_logical(q, 4) == lax.shift_right_logical(b, 4))
    start = dot(ones_where(here & (q < b)), count)
    first = dot(ones_where(here & (q < (b & ~1))), count).astype(jnp.int32)
    base = jnp.minimum(first & ~15, CAP - WINDOW)
    base_ref[...] = base
    shift = (start - base.astype(F32)).astype(BF16)
    spread = ones_where(lax.shift_right_logical(iota((128, 1024), 1), 6) == iota((128, 1024), 0))
    gap = dot(shift, spread)
    col = iota((32, 1024), 1)
    key_ref[...] = jnp.where((col & 63).astype(F32) >= gap, col.astype(F32) - gap, -1.0)


def split_kernel(rows_ref, out_ref):
    for c in range(4):
        out_ref[c] = rows_ref[:, 128 * c : 128 * c + 128]


def select_kernel(half, base_ref, key_ref, rows_ref, list_ref, out_ref):
    g = pl.program_id(0) + 8 * half
    parts = []
    for p in range(16):
        at = pl.multiple_of(base_ref[2 * g, p], 16)
        parts.append(list_ref[p, pl.ds(at, WINDOW), :])
    window = jnp.concatenate(parts, 0)
    meta = rows_ref[:, 128:256].astype(F32)
    key = key_ref[0]
    hot = []
    for t in range(8):
        want = meta[:, t : t + 1] * 64.0 + meta[:, 8 + t : 9 + t]
        hot.append(ones_where(want[0:32] == key[0:1]))
        hot.append(ones_where(want[32:64] == key[1:2]))
    got = dot(jnp.concatenate(hot, 0), window)
    v = rows_ref[:, 0:128].astype(F32)
    v_roll = pltpu.roll(v, 64, 1)
    left = iota((64, 128), 1) < 64
    for t in range(8):
        c = got[64 * t : 64 * t + 64]
        out_ref[0, t] = jnp.where(left, v, pltpu.roll(c, 64, 1)).astype(BF16)
        out_ref[1, t] = jnp.where(left, v_roll, c).astype(BF16)


def combine(parts, words):
    p0, p1, p2, p3 = parts
    total = (p0[...] + p2[...]) + (p1[...] + p3[...])

    def column(a):
        row = jnp.concatenate([total[256 + 2 * a : 257 + 2 * a], total[257 + 2 * a : 258 + 2 * a]], 1)
        return jnp.broadcast_to(row, (128, 256)).T

    count = jnp.where(iota((256, 128), 1) < 64, column(0), column(1))
    return (total[0:256] + words) / (count + 1.0)


def em_kernel(halves, carried, last, *refs):
    refs = list(refs)
    parts = [refs.pop(0) for _ in range(4)] if last else None
    base_ref = refs.pop(0) if carried else None
    x_refs = [refs.pop(0) for _ in halves]
    rows_ref, words_ref, var_ref, out_ref = refs[:4]
    if last:
        new_ref, err_ref = refs[4:6]
        words = combine(parts, words_ref[...])
        new_ref[...] = words
    else:
        words = words_ref[...]
    mat_ref, weight_ref, acc_ref = refs[-3:]
    scale = LOG2E / var_ref[...]
    scaled = words * scale
    rolled = pltpu.roll(scaled, 64, 1)
    left = iota((256, 128), 1) < 64
    biases = []
    for a in range(2):
        x = jnp.where(left, scaled, -rolled) if a == 0 else jnp.where(left, rolled, -scaled)
        hi = x.astype(BF16)
        mat_ref[a, :, 0:128] = hi
        mat_ref[a, :, 128:256] = (x - hi.astype(F32)).astype(BF16)
        mine = left if a == 0 else jnp.logical_not(left)
        biases.append(0.5 * jnp.sum(jnp.where(mine, scaled * words, 0.0), axis=1, keepdims=True))
    for half in halves:
        for c in range(4 * half, 4 * half + 4):
            flipped = rows_ref[128 * c : 128 * c + 128, 128:256].astype(F32).T
            weight_ref[:, 128 * c : 128 * c + 128] = flipped[16:24]
    acc_ref[...] = jnp.zeros_like(acc_ref)
    ones = jnp.ones((TILE, 128), BF16)

    def slots(t, carry):
        for h, half in enumerate(halves):
            for c in range(512 // TILE):
                at = pl.ds(c * TILE, TILE)
                weight = weight_ref[pl.ds(t, 1), pl.ds(512 * half + c * TILE, TILE)]
                error = jnp.zeros((1, TILE), F32)
                for a in range(2):
                    x = x_refs[h][a, t, at, :]
                    s = dot(mat_ref[a], jnp.concatenate([x, x], 1), NT) - biases[a]
                    top = jnp.max(s, axis=0, keepdims=True)
                    e = jnp.exp2(s - top)
                    inv = 1.0 / jnp.sum(e, axis=0, keepdims=True)
                    if last:
                        xf = x.astype(F32)
                        d = xf - pltpu.roll(xf, 64, 1)
                        d2 = d * d
                        hi = d2.astype(BF16)
                        lo = (d2 - hi.astype(F32)).astype(BF16)
                        r2 = dot(jnp.full((8, 256), 0.5, BF16), jnp.concatenate([hi, lo], 1), NT)[0:1]
                        mean = jnp.sum(e * s, axis=0, keepdims=True) * inv
                        error = error + (r2 - mean * (2.0 / scale[0:1, 64 * a : 64 * a + 1]))
                    w = e * (inv * weight)
                    w_hi = w.astype(BF16)
                    w_lo = (w - w_hi.astype(F32)).astype(BF16)
                    tall = jnp.concatenate([x, ones], 1)
                    acc_ref[a] += dot(jnp.concatenate([w_hi, w_lo], 1), jnp.concatenate([tall, tall], 0))
                if last:
                    for i in range(TILE // 256):
                        zb = (512 * half + c * TILE) // 256 + i
                        err_ref[zb, pl.ds(t, 1), :] = error[:, 256 * i : 256 * i + 256]
        return carry

    lax.fori_loop(0, 8, slots, 0)
    diff = [acc_ref[a, :, 0:128] - pltpu.roll(acc_ref[a, :, 0:128], 64, 1) for a in range(2)]
    sums = jnp.where(left, diff[0], -diff[1])
    tail = []
    for a in range(2):
        row = acc_ref[a, :, 128:256].T[0:1]
        tail += [row[:, 0:128], row[:, 128:256]]
    tail = jnp.concatenate(tail + [jnp.zeros((4, 128), F32)], 0)
    if carried:
        sums = sums + base_ref[0:256]
        tail = tail + base_ref[256:264]
    out_ref[0:256] = sums
    out_ref[256:264] = tail


def em(halves, carried, last, args):
    shapes = [jax.ShapeDtypeStruct((264, 128), F32)]
    if last:
        shapes += [jax.ShapeDtypeStruct((256, 128), F32), jax.ShapeDtypeStruct((4, 8, 256), F32)]
    return pl.pallas_call(
        functools.partial(em_kernel, halves, carried, last),
        out_shape=shapes,
        in_specs=[VMEM] * len(args),
        out_specs=[VMEM] * len(shapes),
        scratch_shapes=[
            pltpu.VMEM((2, 256, 256), BF16),
            pltpu.VMEM((8, 1024), F32),
            pltpu.VMEM((2, 256, 256), F32),
        ],
        compiler_params=params(),
        name="em_last" if last else "em_first",
    )(*args)


def update_kernel(p0, p1, p2, p3, words_ref, out_ref):
    out_ref[...] = combine((p0, p1, p2, p3), words_ref[...]).T


def assemble_kernel(z_ref, x0, x1, x2, x3, out_ref):
    for d, x in enumerate((x0, x1, x2, x3)):
        out_ref[(z_ref[0] + (4 - d)) & 3] = x[...]


def shifts(x, axis):
    return [x] + [lax.ppermute(x, axis, [(i, (i + d) % 4) for i in range(4)]) for d in (1, 2, 3)]


def per_device(vectors, owner, local, mask, slot_weight, centroids, codebook, variance):
    z, y = lax.axis_index("z"), lax.axis_index("y")
    me = (z * 4 + y).astype(jnp.int32).reshape(1)
    y1, z1 = y.astype(jnp.int32).reshape(1), z.astype(jnp.int32).reshape(1)
    valid = mask > 0
    owned = jnp.where(valid, owner, -1)

    posting = jnp.where(valid, owner * 8192 + local, -1).T.reshape(1, 2, 128)
    ids = lax.all_to_all(
        jnp.broadcast_to(posting, (128, 2, 128)), ("z", "y", "sub"), 0, 0, tiled=True
    ).reshape(256, 128)

    wanted = pl.pallas_call(
        list_kernel,
        out_shape=[jax.ShapeDtypeStruct((4, CAP), jnp.int32)] * 2,
        in_specs=[SMEM, VMEM],
        out_specs=[VMEM] * 2,
        compiler_params=params(),
        name="lists",
    )(me, ids)

    def fetch(want):
        found = centroids.at[want.reshape(4 * CAP)].get(mode="promise_in_bounds")
        found = pl.pallas_call(
            split_kernel,
            out_shape=jax.ShapeDtypeStruct((4, 4 * CAP, 128), BF16),
            in_specs=[VMEM],
            out_specs=VMEM,
            compiler_params=params(),
            name="split",
        )(found)
        return lax.all_to_all(found.reshape(16, CAP, 128), ("z", "y"), 0, 0, tiled=True)

    lists = [fetch(want) for want in wanted]

    names = jnp.any(owned[:, :, None] == jnp.arange(16)[None, None, :], axis=1)
    upto = jnp.dot(jnp.tril(jnp.ones((32, 32), F32), -1), names.astype(F32))
    rank = jnp.sum(jnp.where(owned[:, :, None] == jnp.arange(16)[None, None, :], upto[:, None, :], 0.0), axis=2)
    weight = slot_weight * mask.astype(slot_weight.dtype)
    meta = jnp.concatenate([owned.astype(BF16), rank.astype(BF16), weight, jnp.zeros((32, 104), BF16)], 1)
    packed = jnp.concatenate(
        [
            vectors.reshape(32, 8, 4, 128).transpose(2, 1, 0, 3).reshape(32, 32, 128),
            jnp.broadcast_to(meta, (32, 32, 128)),
        ],
        2,
    )
    rows = lax.all_to_all(packed, ("z", "sub"), 0, 0, tiled=True).reshape(1024, 256)

    keys, base = pl.pallas_call(
        key_kernel,
        out_shape=(jax.ShapeDtypeStruct((32, 1024), F32), jax.ShapeDtypeStruct((32, 128), jnp.int32)),
        in_specs=[SMEM, VMEM],
        out_specs=(VMEM, VMEM),
        compiler_params=params(),
        name="keys",
    )(y1, ids)
    keys = keys.reshape(16, 2, 1024)

    def select(half):
        return pl.pallas_call(
            functools.partial(select_kernel, half),
            out_shape=jax.ShapeDtypeStruct((2, 8, 512, 128), BF16),
            grid_spec=pltpu.PrefetchScalarGridSpec(
                num_scalar_prefetch=1,
                grid=(8,),
                in_specs=[
                    pl.BlockSpec((1, 2, 1024), lambda g, b: (g + 8 * half, 0, 0)),
                    pl.BlockSpec((64, 256), lambda g, b: (g + 8 * half, 0)),
                    pl.BlockSpec((16, CAP, 128), lambda g, b: (0, 0, 0)),
                ],
                out_specs=pl.BlockSpec((2, 8, 64, 128), lambda g, b: (0, 0, g, 0)),
            ),
            compiler_params=params(),
            name="select",
        )(base, keys, rows, lists[half])

    words = lax.dynamic_slice(codebook, (2 * z, 0, 0), (2, 256, 64)).transpose(1, 0, 2).reshape(256, 128)
    spread = jnp.repeat(lax.dynamic_slice(variance, (2 * z,), (2,)), 64).reshape(1, 128)
    x = [select(0)]
    (part,) = em((0,), False, False, (x[0], rows, words, spread))
    x.append(select(1))
    (part,) = em((1,), True, False, (part, x[1], rows, words, spread))
    part, words, error = em((0, 1), False, True, (*shifts(part, "y"), *x, rows, words, spread))
    turned = pl.pallas_call(
        update_kernel,
        out_shape=jax.ShapeDtypeStruct((128, 256), F32),
        in_specs=[VMEM] * 5,
        out_specs=VMEM,
        name="update",
    )(*shifts(part, "y"), words)
    trained = pl.pallas_call(
        assemble_kernel,
        out_shape=jax.ShapeDtypeStruct((4, 128, 256), F32),
        in_specs=[SMEM] + [VMEM] * 4,
        out_specs=VMEM,
        name="assemble",
    )(z1, *shifts(turned, "z"))
    trained = trained.reshape(8, 64, 256).transpose(0, 2, 1)

    error = jnp.sum(lax.all_to_all(error, "z", 0, 0, tiled=True), axis=0)
    error, _ = lax.optimization_barrier((error, turned))
    error = error.reshape(8, 8, 32).transpose(1, 0, 2)
    error = jnp.sum(lax.all_to_all(error, "sub", 0, 0, tiled=True), axis=0).T
    return trained, error / vectors.shape[1] * mask.astype(F32)


def solution(mesh):
    grid = Mesh(mesh.devices.reshape(4, 4, 8), ("z", "y", "sub"))
    rows = P(("z", "y", "sub"), None)
    return jax.shard_map(
        per_device,
        mesh=grid,
        in_specs=(rows, rows, rows, rows, rows, P(("z", "y"), "sub"), P("sub", None, None), P("sub")),
        out_specs=(P("sub", None, None), rows),
        check_vma=False,
    )
```

time: 204 us -> 174 us (0.85)
  waiting for transfers between devices: 58.8 us -> 29 us
  starting transfers between devices: 37.4 us -> 45.9 us
  blocking collectives: 13.1 us -> 7.97 us
  local copies, waits for them, and re-layouts: 35.6 us -> 33 us
  Pallas kernels: 52.6 us -> 50.3 us
    all_to_all x1 -> x3, waiting for transfers between devices: 42.9 us -> 14.6 us  [the longest x2 13 us: fetch(): lax.all_to_all(found.reshape(16, CAP, 128), ('z', 'y'), 0, 0, tiled=True)]
    all_to_all x1 -> x3, starting transfers between devices: 6.89 us -> 18.5 us  [the longest x2 14.3 us: fetch(): lax.all_to_all(found.reshape(16, CAP, 128), ('z', 'y'), 0, 0, tiled=True)]
    reshape x5 -> x2, local copies, waits for them, and re-layouts: 9.94 us -> 0.15 us  [the longest x1 0.07 us: per_device(): keys = keys.reshape(16, 2, 1024)]
    unnamed x26 -> x40, local copies, waits for them, and re-layouts: 4.57 us -> 10.3 us
    all_to_all x1, blocking collectives: 13.1 us -> 7.97 us  [per_device(): error = jnp.sum(lax.all_to_all(error, 'z', 0, 0, tiled=True), axis=0)]
    ppermute x9, starting transfers between devices: 16.1 us -> 13 us  [shifts(): lax.ppermute(x, axis, [(i, (i + d) % 4) for i in range(4)])]
    pallas_call x7 -> x11, Pallas kernels: 52.6 us -> 50.3 us  [the longest x3 29.7 us: em(): pl.pallas_call(functools.partial(em_kernel, halves, carried, last), out_s...]
    ppermute x9, waiting for transfers between devices: 11.2 us -> 8.93 us  [shifts(): lax.ppermute(x, axis, [(i, (i + d) % 4) for i in range(4)])]
  transfers between devices with their start and end apart: 12 -> 14, of which waited for: 7 -> 9; matrix products, arithmetic and copies ran while one was open for 17% -> 15% of each run, Pallas kernels for 2% -> 10%
where the time goes in v2:
time: 174 us; the launch traced here: 172 us
  Pallas kernels  50.3 us (29%)
  starting transfers between devices  45.9 us (26%)
  local copies, waits for them, and re-layouts  33 us (19%)
  waiting for transfers between devices  29 us (17%)
  blocking collectives  7.97 us (5%)
  other arithmetic  4.54 us (3%)
    pallas_call x3, Pallas kernels, em(): pl.pallas_call(functools.partial(em_kernel, halves, carried, last), out_s...  29.7 us
    gather x2, local copies, waits for them, and re-layouts, fetch(): found = centroids.at[want.reshape(4 * CAP)].get(mode='promise_in_bounds')  19.3 us
    all_to_all x2, starting transfers between devices, fetch(): lax.all_to_all(found.reshape(16, CAP, 128), ('z', 'y'), 0, 0, tiled=True)  14.3 us
    pallas_call x2, Pallas kernels, select(): pl.pallas_call(functools.partial(select_kernel, half), out_shape=jax.Shap...  13.7 us
    ppermute x9, starting transfers between devices, shifts(): lax.ppermute(x, axis, [(i, (i + d) % 4) for i in range(4)])  13 us
    all_to_all x2, waiting for transfers between devices, fetch(): lax.all_to_all(found.reshape(16, CAP, 128), ('z', 'y'), 0, 0, tiled=True)  13 us
    all_to_all x1, starting transfers between devices, per_device(): lax.all_to_all(jnp.broadcast_to(posting, (128, 2, 128)), ('z', 'y', 'sub'...  10.4 us
    unnamed x40, local copies, waits for them, and re-layouts  10.3 us
  transfers between devices with their start and end apart: 14, of which 9 were waited for; matrix products, arithmetic and copies ran while one was open for 15% of the time, Pallas kernels for 10%

profile of v2, /device:TPU:8, one launch (start us, length us, event | category | flops | bytes accessed | tf_op | source)
XLA Modules:
  0.0 171.9 jit_solution(18225055880593064196)
XLA Ops:
  0.6 0.8 fusion.10
  1.4 0.7 select_bitcast_fusion
  2.2 0.7 broadcast_in_dim.49
  2.9 10.4 %all-to-all-start = ((s32[128,2,128]{2,1,0:T(2,128)}), s32[128,2,128]{2,1,0:T(2,128)S(1)}, u32[]{:S(2)}, u32[]{:S(2)}) async-start(s32[128,2,128]{2,1,0:T(2,128)} %broadcast_in_dim.49), calls=%async_computation | async-start | bytes 262144 | tf_op jit(solution)/shard_map/all_to_all | solution.py:271
  13.8 0.7 convert_multiply_fusion
  14.8 1.1 reshape.113
  16.0 0.9 pad_maximum_fusion
  16.9 5.5 %all-to-all-done = s32[128,2,128]{2,1,0:T(2,128)S(1)} async-done(((s32[128,2,128]{2,1,0:T(2,128)}), s32[128,2,128]{2,1,0:T(2,128)S(1)}, u32[]{:S(2)}, u32[]{:S(2)}) %all-to-all-start) | async-done | bytes 131104 | tf_op jit(solution)/shard_map/all_to_all | solution.py:271
  22.4 3.9 %all-to-all-start.1 = ((bf16[32,32,256]{2,1,0:T(8,128)(2,1)}), bf16[32,32,256]{2,1,0:T(8,128)(2,1)S(1)}, u32[]{:S(2)}, u32[]{:S(2)}) async-start(bf16[32,32,256]{2,1,0:T(8,128)(2,1)} %pad_maximum_fusion), calls=%async_computation.1 | async-start | bytes 1048576 | tf_op jit(solution)/shard_map/all_to_all | solution.py:310
  26.3 1.6 lists.1
  27.9 9.3 %gather_fusion = bf16[1536,512]{1,0:T(8,128)(2,1)S(1)} fusion(bf16[8192,512]{1,0:T(8,128)(2,1)} %param.13, s32[2048]{0:T(1024)S(1)} %pad_clamp_fusion.1), kind=kCustom, calls=%fused_computation | custom fusion | bytes 3151872 | tf_op jit(solution)/shard_map/gather | solution.py:285
  37.5 1.1 copy-done.4
  38.7 6.8 %all-to-all-start.2 = ((bf16[16,384,128]{2,1,0:T(8,128)(2,1)}), bf16[16,384,128]{2,1,0:T(8,128)(2,1)S(1)}, u32[]{:S(2)}, u32[]{:S(2)}) async-start(bf16[16,384,128]{2,1,0:T(8,128)(2,1)} %bitcast.35), calls=%async_computation.2 | async-start | bytes 3145728 | tf_op jit(solution)/shard_map/all_to_all | solution.py:294
  45.5 9.9 %gather_fusion.1 = bf16[1536,512]{1,0:T(8,128)(2,1)} fusion(bf16[8192,512]{1,0:T(8,128)(2,1)} %param.13, s32[2048]{0:T(1024)S(1)} %pad_clamp_fusion), kind=kCustom, calls=%fused_computation.1 | custom fusion | bytes 3151872 | tf_op jit(solution)/shard_map/gather | solution.py:285
  55.4 1.4 copy-done.5
  57.1 1.2 copy-done.3
  58.3 9.0 %all-to-all-done.2.list_ref = bf16[16,384,128]{2,1,0:T(8,128)(2,1)S(1)} async-done(((bf16[16,384,128]{2,1,0:T(8,128)(2,1)}), bf16[16,384,128]{2,1,0:T(8,128)(2,1)S(1)}, u32[]{:S(2)}, u32[]{:S(2)}) %all-to-all-start.2) | async-done | bytes 1572896 | tf_op jit(solution)/shard_map/all_to_all | solution.py:294
  67.3 1.2 copy-done.1
  68.4 7.5 %all-to-all-start.3 = ((bf16[16,384,128]{2,1,0:T(8,128)(2,1)}), bf16[16,384,128]{2,1,0:T(8,128)(2,1)}, u32[]{:S(2)}, u32[]{:S(2)}) async-start(bf16[16,384,128]{2,1,0:T(8,128)(2,1)} %bitcast.34), calls=%async_computation.3 | async-start | bytes 3145728 | tf_op jit(solution)/shard_map/all_to_all | solution.py:294
  76.3 0.9 keys.1
  77.8 1.4 copy-done.2
  79.2 6.1 %select.2.refs_0_.refs_4_ = bf16[2,8,512,128]{3,2,1,0:T(8,128)(2,1)S(1)} custom-call(s32[32,128]{1,0:T(8,128)S(1)} %get-tuple-element.10.base_ref, f32[16,2,1024]{2,1,0:T(2,128)S(1)} %reshape.112.key_ref, bf16[1024,256]{1,0:T(8,128)(2,1)S(1)} %bitcast.29, bf16[16,384,128]{2,1,0:T(8,128)(2,1)S(1)} %copy-done.2), custom_call_target="tpu_custom_call" | custom-call | tf_op jit(solution)/shard_map/select/pallas_call | solution.py:323
  85.4 7.4 %em_first.2.refs_0_ = f32[264,128]{1,0:T(8,128)S(1)} custom-call(bf16[2,8,512,128]{3,2,1,0:T(8,128)(2,1)S(1)} %select.2.refs_0_.refs_4_, bf16[1024,256]{1,0:T(8,128)(2,1)S(1)} %bitcast.30, f32[256,128]{1,0:T(8,128)S(1)} %copy.45.refs_2_.refs_3_.refs_7_, f32[1,128]{1,0:T(1,128)S(1)} %reshape_reshape.3.refs_3_.refs_4_.refs_8_), custom_call_target="tpu_custom_call" | custom-call | tf_op jit(solution)/shard_map/em_first/pallas_call | solution.py:235
  92.8 4.1 %all-to-all-done.3.list_ref = bf16[16,384,128]{2,1,0:T(8,128)(2,1)} async-done(((bf16[16,384,128]{2,1,0:T(8,128)(2,1)}), bf16[16,384,128]{2,1,0:T(8,128)(2,1)}, u32[]{:S(2)}, u32[]{:S(2)}) %all-to-all-start.3) | async-done | bytes 1572896 | tf_op jit(solution)/shard_map/all_to_all | solution.py:294
  96.8 0.7 copy-done.9
  97.6 7.6 %select.3.refs_1_.refs_5_ = bf16[2,8,512,128]{3,2,1,0:T(8,128)(2,1)S(1)} custom-call(s32[32,128]{1,0:T(8,128)S(1)} %copy-done.9, f32[16,2,1024]{2,1,0:T(2,128)S(1)} %reshape.112.key_ref, bf16[1024,256]{1,0:T(8,128)(2,1)S(1)} %bitcast.31, bf16[16,384,128]{2,1,0:T(8,128)(2,1)} %all-to-all-done.3.list_ref), custom_call_target="tpu_custom_call" | custom-call | tf_op jit(solution)/shard_map/select/pallas_call | solution.py:323
  105.1 7.3 %em_first.3.refs_0_ = f32[264,128]{1,0:T(8,128)S(1)} custom-call(f32[264,128]{1,0:T(8,128)S(1)} %em_first.2.refs_0_, bf16[2,8,512,128]{3,2,1,0:T(8,128)(2,1)S(1)} %select.3.refs_1_.refs_5_, bf16[1024,256]{1,0:T(8,128)(2,1)S(1)} %bitcast.32, f32[256,128]{1,0:T(8,128)S(1)} %copy.45.refs_2_.refs_3_.refs_7_, f32[1,128]{1,0:T(1,128)S(1)} %reshape_reshape.3.refs_3_.refs_4_.refs_8_), custom_call_target="tpu_custom_call" | custom-call | tf_op jit(solution)/shard_map/em_first/pallas_call | solution.py:235
  112.6 4.3 %collective-permute-start.1 = (f32[264,128]{1,0:T(8,128)S(1)}, f32[264,128]{1,0:T(8,128)S(1)}, u32[]{:S(2)}, u32[]{:S(2)}) collective-permute-start(f32[264,128]{1,0:T(8,128)S(1)} %em_first.3.refs_0_), channel_id=1, source_target_pairs={{0,16},{8,24},{16,0},{24,8},{1,17},{9,25},{17,1},{25,9},{2,18},{10... | collective-permute-start | bytes 405512 | tf_op jit(solution)/shard_map/ppermute | solution.py:260
  116.8 1.5 collective-permute-done.refs_1_
  118.3 2.4 %collective-permute-done.1.refs_2_ = f32[264,128]{1,0:T(8,128)S(1)} collective-permute-done((f32[264,128]{1,0:T(8,128)S(1)}, f32[264,128]{1,0:T(8,128)S(1)}, u32[]{:S(2)}, u32[]{:S(2)}) %collective-permute-start.1) | collective-permute-done | bytes 135200 | tf_op jit(solution)/shard_map/ppermute | solution.py:260
  120.8 1.4 collective-permute-done.2.refs_3_
  122.2 14.9 %em_last.1 = (f32[264,128]{1,0:T(8,128)S(1)}, f32[256,128]{1,0:T(8,128)S(1)}, f32[4,8,256]{2,1,0:T(8,128)S(1)}) custom-call(f32[264,128]{1,0:T(8,128)S(1)} %em_first.3.refs_0_, f32[264,128]{1,0:T(8,128)S(1)} %collective-permute-done.refs_1_, f32[264,128]{1,0:T(8,128)S(1)} %collective-permute-done.1.refs_2_, f32[264,128]{1,0:T(8,128)S(1)} %collective-permute-done.2.refs_3_, ...), custom_call_target="tpu_custom_call" | custom-call | tf_op jit(solution)/shard_map/em_last/pallas_call | solution.py:235
  137.1 0.7 copy-done.7
  138.4 2.6 %collective-permute-start.4 = (f32[264,128]{1,0:T(8,128)S(1)}, f32[264,128]{1,0:T(8,128)S(1)}, u32[]{:S(2)}, u32[]{:S(2)}) collective-permute-start(f32[264,128]{1,0:T(8,128)S(1)} %get-tuple-element.14.p0), channel_id=1, source_target_pairs={{0,16},{8,24},{16,0},{24,8},{1,17},{9,25},{17,1},{25,9},{2,18},{10... | collective-permute-start | bytes 405512 | tf_op jit(solution)/shard_map/ppermute | solution.py:260
  141.0 1.7 %collective-permute-start.5 = (f32[264,128]{1,0:T(8,128)S(1)}, f32[264,128]{1,0:T(8,128)S(1)}, u32[]{:S(2)}, u32[]{:S(2)}) collective-permute-start(f32[264,128]{1,0:T(8,128)S(1)} %get-tuple-element.14.p0), channel_id=1, source_target_pairs={{0,24},{8,0},{16,8},{24,16},{1,25},{9,1},{17,9},{25,17},{2,26},{10... | collective-permute-start | bytes 405512 | tf_op jit(solution)/shard_map/ppermute | solution.py:260
  142.8 8.0 %all_to_all.30 = f32[4,8,256]{2,1,0:T(8,128)S(1)} all-to-all(f32[4,8,256]{2,1,0:T(8,128)S(1)} %get-tuple-element.16), channel_id=1, replica_groups=mesh['z'=4,'y'=4,'sub'=8] {'z'}, dimensions={0} | all-to-all | bytes 65536 | tf_op jit(solution)/shard_map/all_to_all | solution.py:363
  150.8 0.6 copy-done.10
  151.5 2.0 %update.1.x0 = f32[128,256]{1,0:T(8,128)} custom-call(f32[264,128]{1,0:T(8,128)} %copy-done.6, f32[264,128]{1,0:T(8,128)} %copy-done.10, f32[264,128]{1,0:T(8,128)} %copy-done.11, f32[264,128]{1,0:T(8,128)} %copy-done.12, f32[256,128]{1,0:T(8,128)} %copy-done.7), custom_call_target="tpu_custom_call" | custom-call | tf_op jit(solution)/shard_map/update/pallas_call | solution.py:347
  153.6 0.7 reshape.142
  154.3 4.3 %all-to-all-start.5 = ((f32[8,1,256]{2,1,0:T(1,128)}), f32[8,1,256]{2,1,0:T(1,128)S(1)}, u32[]{:S(2)}, u32[]{:S(2)}) async-start(f32[8,1,256]{2,1,0:T(1,128)} %reshape.142), calls=%async_computation.5 | async-start | bytes 16384 | tf_op jit(solution)/shard_map/all_to_all | solution.py:366
  159.1 2.1 %collective-permute-start.7 = (f32[128,256]{1,0:T(8,128)}, f32[128,256]{1,0:T(8,128)S(1)}, u32[]{:S(2)}, u32[]{:S(2)}) collective-permute-start(f32[128,256]{1,0:T(8,128)} %update.1.x0), channel_id=1, source_target_pairs={{0,64},{32,96},{64,0},{96,32},{1,65},{33,97},{65,1},{97,33},{2,66}... | collective-permute-start | bytes 393224 | tf_op jit(solution)/shard_map/ppermute | solution.py:260
  161.2 1.1 collective-permute-start.8
  162.3 1.6 all-to-all-done.5
  164.4 0.7 reduce.4
  165.2 0.6 bitcast_multiply_fusion
  165.8 2.9 %collective-permute-done.6.x1 = f32[128,256]{1,0:T(8,128)S(1)} collective-permute-done((f32[128,256]{1,0:T(8,128)}, f32[128,256]{1,0:T(8,128)S(1)}, u32[]{:S(2)}, u32[]{:S(2)}) %collective-permute-start.6) | collective-permute-done | bytes 131104 | tf_op jit(solution)/shard_map/ppermute | solution.py:260
  168.7 0.6 collective-permute-done.8.x3
  170.0 1.9 %assemble.1 = f32[4,128,256]{2,1,0:T(8,128)} custom-call(s32[1]{0:T(128)} %bitcast.z_ref, f32[128,256]{1,0:T(8,128)} %update.1.x0, f32[128,256]{1,0:T(8,128)} %copy-done.13, f32[128,256]{1,0:T(8,128)} %copy-done.14, f32[128,256]{1,0:T(8,128)} %copy-done.15), custom_call_target="tpu_custom_call" | custom-call | tf_op jit(solution)/shard_map/assemble/pallas_call | solution.py:354
  (70 shorter events, 5.2 us)
Async XLA Ops:
  0.6 75.3 %copy-start = (f32[8,256,64]{1,2,0:T(8,128)S(1)}, f32[8,256,64]{1,2,0:T(8,128)}, u32[]{:S(2)}) copy-start(f32[8,256,64]{1,2,0:T(8,128)} %param.14) | copy-start | bytes 1572868
  2.9 19.5 %all-to-all-start = ((s32[128,2,128]{2,1,0:T(2,128)}), s32[128,2,128]{2,1,0:T(2,128)S(1)}, u32[]{:S(2)}, u32[]{:S(2)}) async-start(s32[128,2,128]{2,1,0:T(2,128)} %broadcast_in_dim.49), calls=%async_computation | async-start | bytes 262144 | tf_op jit(solution)/shard_map/all_to_all | solution.py:271
  22.4 16.3 %all-to-all-start.1 = ((bf16[32,32,256]{2,1,0:T(8,128)(2,1)}), bf16[32,32,256]{2,1,0:T(8,128)(2,1)S(1)}, u32[]{:S(2)}, u32[]{:S(2)}) async-start(bf16[32,32,256]{2,1,0:T(8,128)(2,1)} %pad_maximum_fusion), calls=%async_computation.1 | async-start | bytes 1048576 | tf_op jit(solution)/shard_map/all_to_all | solution.py:310
  37.5 1.1 copy-start.4
  38.7 28.6 %all-to-all-start.2 = ((bf16[16,384,128]{2,1,0:T(8,128)(2,1)}), bf16[16,384,128]{2,1,0:T(8,128)(2,1)S(1)}, u32[]{:S(2)}, u32[]{:S(2)}) async-start(bf16[16,384,128]{2,1,0:T(8,128)(2,1)} %bitcast.35), calls=%async_computation.2 | async-start | bytes 3145728 | tf_op jit(solution)/shard_map/all_to_all | solution.py:294
  55.4 1.4 copy-start.5
  57.1 1.2 copy-start.3
  67.3 1.2 copy-start.1
  67.3 8.8 %copy-start.17 = (f32[8]{0:T(128)S(1)}, f32[8]{0:T(128)}, u32[]{:S(2)}) copy-start(f32[8]{0:T(128)} %param.15) | copy-start | bytes 100
  68.4 28.4 %all-to-all-start.3 = ((bf16[16,384,128]{2,1,0:T(8,128)(2,1)}), bf16[16,384,128]{2,1,0:T(8,128)(2,1)}, u32[]{:S(2)}, u32[]{:S(2)}) async-start(bf16[16,384,128]{2,1,0:T(8,128)(2,1)} %bitcast.34), calls=%async_computation.3 | async-start | bytes 3145728 | tf_op jit(solution)/shard_map/all_to_all | solution.py:294
  77.2 0.6 copy-start.8
  77.8 1.4 copy-start.2
  96.8 0.7 copy-start.9
  112.5 52.7 %copy-start.16 = (s32[32,8]{0,1:T(8,128)S(1)}, s32[32,8]{0,1:T(8,128)}, u32[]{:S(2)}) copy-start(s32[32,8]{0,1:T(8,128)} %param.11) | copy-start | bytes 3076
  112.5 5.9 %collective-permute-start = (f32[264,128]{1,0:T(8,128)S(1)}, f32[264,128]{1,0:T(8,128)S(1)}, u32[]{:S(2)}, u32[]{:S(2)}) collective-permute-start(f32[264,128]{1,0:T(8,128)S(1)} %em_first.3.refs_0_), channel_id=1, source_target_pairs={{0,8},{8,16},{16,24},{24,0},{1,9},{9,17},{17,25},{25,1},{2,10},{10... | collective-permute-start | bytes 405512 | tf_op jit(solution)/shard_map/ppermute | solution.py:260
  112.6 8.2 %collective-permute-start.1 = (f32[264,128]{1,0:T(8,128)S(1)}, f32[264,128]{1,0:T(8,128)S(1)}, u32[]{:S(2)}, u32[]{:S(2)}) collective-permute-start(f32[264,128]{1,0:T(8,128)S(1)} %em_first.3.refs_0_), channel_id=1, source_target_pairs={{0,16},{8,24},{16,0},{24,8},{1,17},{9,25},{17,1},{25,9},{2,18},{10... | collective-permute-start | bytes 405512 | tf_op jit(solution)/shard_map/ppermute | solution.py:260
  116.8 5.4 %collective-permute-start.2 = (f32[264,128]{1,0:T(8,128)S(1)}, f32[264,128]{1,0:T(8,128)S(1)}, u32[]{:S(2)}, u32[]{:S(2)}) collective-permute-start(f32[264,128]{1,0:T(8,128)S(1)} %em_first.3.refs_0_), channel_id=1, source_target_pairs={{0,24},{8,0},{16,8},{24,16},{1,25},{9,1},{17,9},{25,17},{2,26},{10... | collective-permute-start | bytes 405512 | tf_op jit(solution)/shard_map/ppermute | solution.py:260
  137.1 0.7 copy-start.7
  137.8 13.0 %copy-start.6 = (f32[264,128]{1,0:T(8,128)}, f32[264,128]{1,0:T(8,128)S(1)}, u32[]{:S(2)}) copy-start(f32[264,128]{1,0:T(8,128)S(1)} %get-tuple-element.14.p0) | copy-start | bytes 405508
  137.8 12.9 %collective-permute-start.3 = (f32[264,128]{1,0:T(8,128)S(1)}, f32[264,128]{1,0:T(8,128)S(1)}, u32[]{:S(2)}, u32[]{:S(2)}) collective-permute-start(f32[264,128]{1,0:T(8,128)S(1)} %get-tuple-element.14.p0), channel_id=1, source_target_pairs={{0,8},{8,16},{16,24},{24,0},{1,9},{9,17},{17,25},{25,1},{2,10},{10... | collective-permute-start | bytes 405512 | tf_op jit(solution)/shard_map/ppermute | solution.py:260
  138.4 12.4 %collective-permute-start.4 = (f32[264,128]{1,0:T(8,128)S(1)}, f32[264,128]{1,0:T(8,128)S(1)}, u32[]{:S(2)}, u32[]{:S(2)}) collective-permute-start(f32[264,128]{1,0:T(8,128)S(1)} %get-tuple-element.14.p0), channel_id=1, source_target_pairs={{0,16},{8,24},{16,0},{24,8},{1,17},{9,25},{17,1},{25,9},{2,18},{10... | collective-permute-start | bytes 405512 | tf_op jit(solution)/shard_map/ppermute | solution.py:260
  141.0 9.8 %collective-permute-start.5 = (f32[264,128]{1,0:T(8,128)S(1)}, f32[264,128]{1,0:T(8,128)S(1)}, u32[]{:S(2)}, u32[]{:S(2)}) collective-permute-start(f32[264,128]{1,0:T(8,128)S(1)} %get-tuple-element.14.p0), channel_id=1, source_target_pairs={{0,24},{8,0},{16,8},{24,16},{1,25},{9,1},{17,9},{25,17},{2,26},{10... | collective-permute-start | bytes 405512 | tf_op jit(solution)/shard_map/ppermute | solution.py:260
  150.7 0.6 copy-start.10
  150.8 0.7 copy-start.11
  150.8 0.7 copy-start.12
  154.3 9.6 %all-to-all-start.5 = ((f32[8,1,256]{2,1,0:T(1,128)}), f32[8,1,256]{2,1,0:T(1,128)S(1)}, u32[]{:S(2)}, u32[]{:S(2)}) async-start(f32[8,1,256]{2,1,0:T(1,128)} %reshape.142), calls=%async_computation.5 | async-start | bytes 16384 | tf_op jit(solution)/shard_map/all_to_all | solution.py:366
  158.6 10.1 %collective-permute-start.6 = (f32[128,256]{1,0:T(8,128)}, f32[128,256]{1,0:T(8,128)S(1)}, u32[]{:S(2)}, u32[]{:S(2)}) collective-permute-start(f32[128,256]{1,0:T(8,128)} %update.1.x0), channel_id=1, source_target_pairs={{0,32},{32,64},{64,96},{96,0},{1,33},{33,65},{65,97},{97,1},{2,34}... | collective-permute-start | bytes 393224 | tf_op jit(solution)/shard_map/ppermute | solution.py:260
  159.1 9.6 %collective-permute-start.7 = (f32[128,256]{1,0:T(8,128)}, f32[128,256]{1,0:T(8,128)S(1)}, u32[]{:S(2)}, u32[]{:S(2)}) collective-permute-start(f32[128,256]{1,0:T(8,128)} %update.1.x0), channel_id=1, source_target_pairs={{0,64},{32,96},{64,0},{96,32},{1,65},{33,97},{65,1},{97,33},{2,66}... | collective-permute-start | bytes 393224 | tf_op jit(solution)/shard_map/ppermute | solution.py:260
  161.2 8.1 %collective-permute-start.8 = (f32[128,256]{1,0:T(8,128)}, f32[128,256]{1,0:T(8,128)S(1)}, u32[]{:S(2)}, u32[]{:S(2)}) collective-permute-start(f32[128,256]{1,0:T(8,128)} %update.1.x0), channel_id=1, source_target_pairs={{0,96},{32,0},{64,32},{96,64},{1,97},{33,1},{65,33},{97,65},{2,98}... | collective-permute-start | bytes 393224 | tf_op jit(solution)/shard_map/ppermute | solution.py:260
  168.7 0.6 copy-start.13
  168.7 0.7 copy-start.14
  169.3 0.6 copy-start.15

commit v3 on v2

--- a/solution.py
+++ b/solution.py
@@ -14,8 +14,8 @@
 BF16 = jnp.bfloat16
 NT = (((1,), (1,)), ((), ()))
 NN = (((1,), (0,)), ((), ()))
-WINDOW = 64
-TILE = 512
+WINDOW = 32
+TILE = 1024
 CAP = 384
 
 
@@ -98,14 +98,13 @@
     b = iota((32, 256), 0)
     here = (y == me_ref[0]) & (lax.shift_right_logical(q, 4) == lax.shift_right_logical(b, 4))
     start = dot(ones_where(here & (q < b)), count)
-    first = dot(ones_where(here & (q < (b & ~1))), count).astype(jnp.int32)
-    base = jnp.minimum(first & ~15, CAP - WINDOW)
+    base = jnp.minimum(start.astype(jnp.int32) & ~7, CAP - WINDOW)
     base_ref[...] = base
     shift = (start - base.astype(F32)).astype(BF16)
-    spread = ones_where(lax.shift_right_logical(iota((128, 1024), 1), 6) == iota((128, 1024), 0))
+    spread = ones_where(lax.shift_right_logical(iota((128, 512), 1), 5) == iota((128, 512), 0))
     gap = dot(shift, spread)
-    col = iota((32, 1024), 1)
-    key_ref[...] = jnp.where((col & 63).astype(F32) >= gap, col.astype(F32) - gap, -1.0)
+    col = iota((32, 512), 1)
+    key_ref[...] = jnp.where((col & 31).astype(F32) >= gap, col.astype(F32) - gap, -1.0)
 
 
 def split_kernel(rows_ref, out_ref):
@@ -115,26 +114,26 @@
 
 def select_kernel(half, base_ref, key_ref, rows_ref, list_ref, out_ref):
     g = pl.program_id(0) + 8 * half
-    parts = []
-    for p in range(16):
-        at = pl.multiple_of(base_ref[2 * g, p], 16)
-        parts.append(list_ref[p, pl.ds(at, WINDOW), :])
-    window = jnp.concatenate(parts, 0)
     meta = rows_ref[:, 128:256].astype(F32)
-    key = key_ref[0]
-    hot = []
-    for t in range(8):
-        want = meta[:, t : t + 1] * 64.0 + meta[:, 8 + t : 9 + t]
-        hot.append(ones_where(want[0:32] == key[0:1]))
-        hot.append(ones_where(want[32:64] == key[1:2]))
-    got = dot(jnp.concatenate(hot, 0), window)
     v = rows_ref[:, 0:128].astype(F32)
     v_roll = pltpu.roll(v, 64, 1)
-    left = iota((64, 128), 1) < 64
-    for t in range(8):
-        c = got[64 * t : 64 * t + 64]
-        out_ref[0, t] = jnp.where(left, v, pltpu.roll(c, 64, 1)).astype(BF16)
-        out_ref[1, t] = jnp.where(left, v_roll, c).astype(BF16)
+    left = iota((32, 128), 1) < 64
+    for b in range(2):
+        parts = []
+        for p in range(16):
+            at = pl.multiple_of(base_ref[2 * g + b, p], 8)
+            parts.append(list_ref[p, pl.ds(at, WINDOW), :])
+        key = key_ref[0, b : b + 1]
+        own = slice(32 * b, 32 * b + 32)
+        hot = []
+        for t in range(8):
+            want = meta[own, t : t + 1] * float(WINDOW) + meta[own, 8 + t : 9 + t]
+            hot.append(ones_where(want == key))
+        got = dot(jnp.concatenate(hot, 0), jnp.concatenate(parts, 0))
+        for t in range(8):
+            c = got[32 * t : 32 * t + 32]
+            out_ref[0, t, own] = jnp.where(left, v[own], pltpu.roll(c, 64, 1)).astype(BF16)
+            out_ref[1, t, own] = jnp.where(left, v_roll[own], c).astype(BF16)
 
 
 def combine(parts, words):
@@ -161,7 +160,7 @@
         new_ref[...] = words
     else:
         words = words_ref[...]
-    mat_ref, weight_ref, acc_ref = refs[-3:]
+    mat_ref, weight_ref, acc_ref, slot_ref = refs[-4:]
     scale = LOG2E / var_ref[...]
     scaled = words * scale
     rolled = pltpu.roll(scaled, 64, 1)
@@ -174,46 +173,52 @@
         mat_ref[a, :, 128:256] = (x - hi.astype(F32)).astype(BF16)
         mine = left if a == 0 else jnp.logical_not(left)
         biases.append(0.5 * jnp.sum(jnp.where(mine, scaled * words, 0.0), axis=1, keepdims=True))
-    for half in halves:
-        for c in range(4 * half, 4 * half + 4):
-            flipped = rows_ref[128 * c : 128 * c + 128, 128:256].astype(F32).T
-            weight_ref[:, 128 * c : 128 * c + 128] = flipped[16:24]
+    for h, half in enumerate(halves):
+        for c in range(4):
+            flipped = rows_ref[512 * half + 128 * c : 512 * half + 128 * c + 128, 128:256].astype(F32).T
+            for t in range(8):
+                at = 512 * t + 128 * c
+                weight_ref[h : h + 1, at : at + 128] = flipped[16 + t : 17 + t]
     acc_ref[...] = jnp.zeros_like(acc_ref)
     ones = jnp.ones((TILE, 128), BF16)
 
-    def slots(t, carry):
+    def slots(i, carry):
         for h, half in enumerate(halves):
-            for c in range(512 // TILE):
-                at = pl.ds(c * TILE, TILE)
-                weight = weight_ref[pl.ds(t, 1), pl.ds(512 * half + c * TILE, TILE)]
-                error = jnp.zeros((1, TILE), F32)
-                for a in range(2):
-                    x = x_refs[h][a, t, at, :]
-                    s = dot(mat_ref[a], jnp.concatenate([x, x], 1), NT) - biases[a]
-                    top = jnp.max(s, axis=0, keepdims=True)
-                    e = jnp.exp2(s - top)
-                    inv = 1.0 / jnp.sum(e, axis=0, keepdims=True)
-                    if last:
-                        xf = x.astype(F32)
-                        d = xf - pltpu.roll(xf, 64, 1)
-                        d2 = d * d
-                        hi = d2.astype(BF16)
-                        lo = (d2 - hi.astype(F32)).astype(BF16)
-                        r2 = dot(jnp.full((8, 256), 0.5, BF16), jnp.concatenate([hi, lo], 1), NT)[0:1]
-                        mean = jnp.sum(e * s, axis=0, keepdims=True) * inv
-                        error = error + (r2 - mean * (2.0 / scale[0:1, 64 * a : 64 * a + 1]))
-                    w = e * (inv * weight)
-                    w_hi = w.astype(BF16)
-                    w_lo = (w - w_hi.astype(F32)).astype(BF16)
-                    tall = jnp.concatenate([x, ones], 1)
-                    acc_ref[a] += dot(jnp.concatenate([w_hi, w_lo], 1), jnp.concatenate([tall, tall], 0))
+            at = pl.ds(pl.multiple_of(i * TILE, TILE), TILE)
+            weight = weight_ref[h : h + 1, at]
+            xs = [x_refs[h][a, at, :] for a in range(2)]
+            if last:
+                d2 = jnp.zeros((TILE, 128), F32)
+                for x in xs:
+                    d = x.astype(F32)
+                    d = d - pltpu.roll(d, 64, 1)
+                    d2 = d2 + d * d
+                error = [jnp.sum(d2[128 * k : 128 * k + 128].T, axis=0, keepdims=True) for k in range(TILE // 128)]
+                error = 0.5 * jnp.concatenate(error, 1)
+            for a, x in enumerate(xs):
+                s = dot(mat_ref[a], jnp.concatenate([x, x], 1), NT) - biases[a]
+                top = jnp.max(s, axis=0, keepdims=True)
+                e = jnp.exp2(s - top)
+                inv = 1.0 / jnp.sum(e, axis=0, keepdims=True)
                 if last:
-                    for i in range(TILE // 256):
-                        zb = (512 * half + c * TILE) // 256 + i
-                        err_ref[zb, pl.ds(t, 1), :] = error[:, 256 * i : 256 * i + 256]
+                    mean = jnp.sum(e * s, axis=0, keepdims=True) * inv
+                    error = error - mean * (2.0 / scale[0:1, 64 * a : 64 * a + 1])
+                w = e * (inv * weight)
+                w_hi = w.astype(BF16)
+                w_lo = (w - w_hi.astype(F32)).astype(BF16)
+                got = dot(jnp.concatenate([w_hi, w_lo], 0), jnp.concatenate([x, ones], 1))
+                acc_ref[a] += got[0:256] + got[256:512]
+            if last:
+                for j in range(TILE // 512):
+                    t = i * (TILE // 512) + j
+                    slot_ref[pl.ds(t, 1), 512 * half : 512 * half + 512] = error[:, 512 * j : 512 * j + 512]
         return carry
 
-    lax.fori_loop(0, 8, slots, 0)
+    lax.fori_loop(0, 4096 // TILE, slots, 0)
+    if last:
+        for sd in range(8):
+            pieces = [slot_ref[:, 32 * (8 * zd + sd) : 32 * (8 * zd + sd) + 32] for zd in range(4)]
+            err_ref[sd] = jnp.concatenate(pieces, 1)
     diff = [acc_ref[a, :, 0:128] - pltpu.roll(acc_ref[a, :, 0:128], 64, 1) for a in range(2)]
     sums = jnp.where(left, diff[0], -diff[1])
     tail = []
@@ -231,7 +236,7 @@
 def em(halves, carried, last, args):
     shapes = [jax.ShapeDtypeStruct((264, 128), F32)]
     if last:
-        shapes += [jax.ShapeDtypeStruct((256, 128), F32), jax.ShapeDtypeStruct((4, 8, 256), F32)]
+        shapes += [jax.ShapeDtypeStruct((256, 128), F32), jax.ShapeDtypeStruct((8, 8, 128), F32)]
     return pl.pallas_call(
         functools.partial(em_kernel, halves, carried, last),
         out_shape=shapes,
@@ -239,25 +244,37 @@
         out_specs=[VMEM] * len(shapes),
         scratch_shapes=[
             pltpu.VMEM((2, 256, 256), BF16),
+            pltpu.VMEM((len(halves), 4096), F32),
+            pltpu.VMEM((2, 256, 256), F32),
             pltpu.VMEM((8, 1024), F32),
-            pltpu.VMEM((2, 256, 256), F32),
         ],
         compiler_params=params(),
         name="em_last" if last else "em_first",
     )(*args)
 
 
-def update_kernel(p0, p1, p2, p3, words_ref, out_ref):
-    out_ref[...] = combine((p0, p1, p2, p3), words_ref[...]).T
-
-
-def assemble_kernel(z_ref, x0, x1, x2, x3, out_ref):
+def update_kernel(p0, p1, p2, p3, words_ref, err_ref, out_ref):
+    out_ref[0:128] = combine((p0, p1, p2, p3), words_ref[...]).T
+    total = err_ref[0]
+    for s in range(1, 8):
+        total = total + err_ref[s]
+    out_ref[128:136] = jnp.concatenate([total, total], 1)
+
+
+def assemble_kernel(z_ref, x0, x1, x2, x3, keep_ref, out_ref, err_ref):
     for d, x in enumerate((x0, x1, x2, x3)):
-        out_ref[(z_ref[0] + (4 - d)) & 3] = x[...]
+        out_ref[(z_ref[0] + (4 - d)) & 3] = x[0:128]
+    error = (x0[128:136, 0:128] + x1[128:136, 0:128]) + (x2[128:136, 0:128] + x3[128:136, 0:128])
+    error = pltpu.roll(error, (128 - 32 * z_ref[0]) & 127, 1)
+    err_ref[...] = error[:, 0:32] * keep_ref[...]
+
+
+def turn(d):
+    return [(i, (i + d) % 4) for i in range(4)]
 
 
 def shifts(x, axis):
-    return [x] + [lax.ppermute(x, axis, [(i, (i + d) % 4) for i in range(4)]) for d in (1, 2, 3)]
+    return [x] + [lax.ppermute(x, axis, turn(d)) for d in (1, 2, 3)]
 
 
 def per_device(vectors, owner, local, mask, slot_weight, centroids, codebook, variance):
@@ -311,13 +328,13 @@
 
     keys, base = pl.pallas_call(
         key_kernel,
-        out_shape=(jax.ShapeDtypeStruct((32, 1024), F32), jax.ShapeDtypeStruct((32, 128), jnp.int32)),
+        out_shape=(jax.ShapeDtypeStruct((32, 512), F32), jax.ShapeDtypeStruct((32, 128), jnp.int32)),
         in_specs=[SMEM, VMEM],
         out_specs=(VMEM, VMEM),
         compiler_params=params(),
         name="keys",
     )(y1, ids)
-    keys = keys.reshape(16, 2, 1024)
+    keys = keys.reshape(16, 2, 512)
 
     def select(half):
         return pl.pallas_call(
@@ -327,7 +344,7 @@
                 num_scalar_prefetch=1,
                 grid=(8,),
                 in_specs=[
-                    pl.BlockSpec((1, 2, 1024), lambda g, b: (g + 8 * half, 0, 0)),
+                    pl.BlockSpec((1, 2, 512), lambda g, b: (g + 8 * half, 0, 0)),
                     pl.BlockSpec((64, 256), lambda g, b: (g + 8 * half, 0)),
                     pl.BlockSpec((16, CAP, 128), lambda g, b: (0, 0, 0)),
                 ],
@@ -335,7 +352,7 @@
             ),
             compiler_params=params(),
             name="select",
-        )(base, keys, rows, lists[half])
+        )(base, keys, rows, lists[half]).reshape(2, 4096, 128)
 
     words = lax.dynamic_slice(codebook, (2 * z, 0, 0), (2, 256, 64)).transpose(1, 0, 2).reshape(256, 128)
     spread = jnp.repeat(lax.dynamic_slice(variance, (2 * z,), (2,)), 64).reshape(1, 128)
@@ -344,27 +361,23 @@
     x.append(select(1))
     (part,) = em((1,), True, False, (part, x[1], rows, words, spread))
     part, words, error = em((0, 1), False, True, (*shifts(part, "y"), *x, rows, words, spread))
+    error = lax.all_to_all(error, "sub", 0, 0, tiled=True)
     turned = pl.pallas_call(
         update_kernel,
-        out_shape=jax.ShapeDtypeStruct((128, 256), F32),
-        in_specs=[VMEM] * 5,
+        out_shape=jax.ShapeDtypeStruct((136, 256), F32),
+        in_specs=[VMEM] * 6,
         out_specs=VMEM,
         name="update",
-    )(*shifts(part, "y"), words)
-    trained = pl.pallas_call(
+    )(*shifts(part, "y"), words, error)
+    keep = mask.T.astype(F32) / vectors.shape[1]
+    trained, error = pl.pallas_call(
         assemble_kernel,
-        out_shape=jax.ShapeDtypeStruct((4, 128, 256), F32),
-        in_specs=[SMEM] + [VMEM] * 4,
-        out_specs=VMEM,
+        out_shape=[jax.ShapeDtypeStruct((4, 128, 256), F32), jax.ShapeDtypeStruct((8, 32), F32)],
+        in_specs=[SMEM] + [VMEM] * 5,
+        out_specs=[VMEM] * 2,
         name="assemble",
-    )(z1, *shifts(turned, "z"))
-    trained = trained.reshape(8, 64, 256).transpose(0, 2, 1)
-
-    error = jnp.sum(lax.all_to_all(error, "z", 0, 0, tiled=True), axis=0)
-    error, _ = lax.optimization_barrier((error, turned))
-    error = error.reshape(8, 8, 32).transpose(1, 0, 2)
-    error = jnp.sum(lax.all_to_all(error, "sub", 0, 0, tiled=True), axis=0).T
-    return trained, error / vectors.shape[1] * mask.astype(F32)
+    )(z1, *shifts(turned, "z"), keep)
+    return trained.reshape(8, 64, 256).transpose(0, 2, 1), error.T
 
 
 def solution(mesh):

time: 174 us -> 164 us (0.943)
  Pallas kernels: 50.3 us -> 44.1 us
  starting transfers between devices: 45.9 us -> 42 us
  waiting for transfers between devices: 29 us -> 32.5 us
  local copies, waits for them, and re-layouts: 33 us -> 30.4 us
    all_to_all x1 -> x0, starting transfers between devices: 4.27 us -> none  [per_device(): error = jnp.sum(lax.all_to_all(error, 'sub', 0, 0, tiled=True), axis=0).T]
    pallas_call x3, Pallas kernels: 29.7 us -> 25.4 us  [em(): pl.pallas_call(functools.partial(em_kernel, halves, carried, last), out_s...]
    all_to_all x2, waiting for transfers between devices: 13 us -> 16 us  [fetch(): lax.all_to_all(found.reshape(16, CAP, 128), ('z', 'y'), 0, 0, tiled=True)]
    ppermute x9, waiting for transfers between devices: 8.93 us -> 11 us  [shifts(): return [x] + [lax.ppermute(x, axis, turn(d)) for d in (1, 2, 3)]]
    pallas_call x2, Pallas kernels: 13.7 us -> 11.7 us  [select(): pl.pallas_call(functools.partial(select_kernel, half), out_shape=jax.Shap...]
    unnamed x40 -> x34, local copies, waits for them, and re-layouts: 10.3 us -> 8.35 us
  transfers between devices with their start and end apart: 14 -> 13, of which waited for: 9 -> 8; matrix products, arithmetic and copies ran while one was open for 15% -> 15% of each run, Pallas kernels for 10% -> 9%
where the time goes in v3:
time: 164 us
  Pallas kernels  44.1 us (27%)
  starting transfers between devices  42 us (26%)
  waiting for transfers between devices  32.5 us (20%)
  local copies, waits for them, and re-layouts  30.4 us (19%)
  blocking collectives  9.61 us (6%)
  other arithmetic  3.85 us (2%)
    pallas_call x3, Pallas kernels, em(): pl.pallas_call(functools.partial(em_kernel, halves, carried, last), out_s...  25.4 us
    gather x2, local copies, waits for them, and re-layouts, fetch(): found = centroids.at[want.reshape(4 * CAP)].get(mode='promise_in_bounds')  19.3 us
    all_to_all x2, waiting for transfers between devices, fetch(): lax.all_to_all(found.reshape(16, CAP, 128), ('z', 'y'), 0, 0, tiled=True)  16 us
    all_to_all x2, starting transfers between devices, fetch(): lax.all_to_all(found.reshape(16, CAP, 128), ('z', 'y'), 0, 0, tiled=True)  14.3 us
    ppermute x9, starting transfers between devices, shifts(): return [x] + [lax.ppermute(x, axis, turn(d)) for d in (1, 2, 3)]  13.4 us
    pallas_call x2, Pallas kernels, select(): pl.pallas_call(functools.partial(select_kernel, half), out_shape=jax.Shap...  11.7 us
    ppermute x9, waiting for transfers between devices, shifts(): return [x] + [lax.ppermute(x, axis, turn(d)) for d in (1, 2, 3)]  11 us
    all_to_all x1, starting transfers between devices, per_device(): lax.all_to_all(jnp.broadcast_to(posting, (128, 2, 128)), ('z', 'y', 'sub'...  10.4 us
  transfers between devices with their start and end apart: 13, of which 8 were waited for; matrix products, arithmetic and copies ran while one was open for 15% of the time, Pallas kernels for 9%

profile of v3, /device:TPU:8, one launch (start us, length us, event | category | flops | bytes accessed | tf_op | source)
XLA Modules:
  0.0 163.6 jit_solution(7862130603639951173)
XLA Ops:
  0.6 0.8 fusion.10
  1.4 0.7 select_bitcast_fusion
  2.2 0.7 broadcast_in_dim.49
  2.9 10.4 %all-to-all-start = ((s32[128,2,128]{2,1,0:T(2,128)}), s32[128,2,128]{2,1,0:T(2,128)S(1)}, u32[]{:S(2)}, u32[]{:S(2)}) async-start(s32[128,2,128]{2,1,0:T(2,128)} %broadcast_in_dim.49), calls=%async_computation | async-start | bytes 262144 | tf_op jit(solution)/shard_map/all_to_all | solution.py:288
  13.8 0.7 convert_multiply_fusion
  14.8 1.1 reshape.116
  16.0 0.9 pad_maximum_fusion
  16.9 5.5 %all-to-all-done = s32[128,2,128]{2,1,0:T(2,128)S(1)} async-done(((s32[128,2,128]{2,1,0:T(2,128)}), s32[128,2,128]{2,1,0:T(2,128)S(1)}, u32[]{:S(2)}, u32[]{:S(2)}) %all-to-all-start) | async-done | bytes 131104 | tf_op jit(solution)/shard_map/all_to_all | solution.py:288
  22.4 3.9 %all-to-all-start.1 = ((bf16[32,32,256]{2,1,0:T(8,128)(2,1)}), bf16[32,32,256]{2,1,0:T(8,128)(2,1)S(1)}, u32[]{:S(2)}, u32[]{:S(2)}) async-start(bf16[32,32,256]{2,1,0:T(8,128)(2,1)} %pad_maximum_fusion), calls=%async_computation.1 | async-start | bytes 1048576 | tf_op jit(solution)/shard_map/all_to_all | solution.py:327
  26.3 1.6 lists.1
  27.9 9.3 %gather_fusion = bf16[1536,512]{1,0:T(8,128)(2,1)S(1)} fusion(bf16[8192,512]{1,0:T(8,128)(2,1)} %param.13, s32[2048]{0:T(1024)S(1)} %pad_clamp_fusion.1), kind=kCustom, calls=%fused_computation | custom fusion | bytes 3151872 | tf_op jit(solution)/shard_map/gather | solution.py:302
  37.3 0.3 split.2
  37.5 1.1 copy-done.4
  38.7 6.8 %all-to-all-start.2 = ((bf16[16,384,128]{2,1,0:T(8,128)(2,1)}), bf16[16,384,128]{2,1,0:T(8,128)(2,1)S(1)}, u32[]{:S(2)}, u32[]{:S(2)}) async-start(bf16[16,384,128]{2,1,0:T(8,128)(2,1)} %bitcast.41), calls=%async_computation.2 | async-start | bytes 3145728 | tf_op jit(solution)/shard_map/all_to_all | solution.py:311
  45.5 10.0 %gather_fusion.1 = bf16[1536,512]{1,0:T(8,128)(2,1)} fusion(bf16[8192,512]{1,0:T(8,128)(2,1)} %param.13, s32[2048]{0:T(1024)S(1)} %pad_clamp_fusion), kind=kCustom, calls=%fused_computation.1 | custom fusion | bytes 3151872 | tf_op jit(solution)/shard_map/gather | solution.py:302
  55.4 1.4 copy-done.5
  56.9 0.3 split.3
  57.1 1.2 copy-done.3
  58.3 8.9 %all-to-all-done.2.list_ref = bf16[16,384,128]{2,1,0:T(8,128)(2,1)S(1)} async-done(((bf16[16,384,128]{2,1,0:T(8,128)(2,1)}), bf16[16,384,128]{2,1,0:T(8,128)(2,1)S(1)}, u32[]{:S(2)}, u32[]{:S(2)}) %all-to-all-start.2) | async-done | bytes 1572896 | tf_op jit(solution)/shard_map/all_to_all | solution.py:311
  67.3 1.2 copy-done.1
  68.4 7.5 %all-to-all-start.3 = ((bf16[16,384,128]{2,1,0:T(8,128)(2,1)}), bf16[16,384,128]{2,1,0:T(8,128)(2,1)}, u32[]{:S(2)}, u32[]{:S(2)}) async-start(bf16[16,384,128]{2,1,0:T(8,128)(2,1)} %bitcast.40), calls=%async_computation.3 | async-start | bytes 3145728 | tf_op jit(solution)/shard_map/all_to_all | solution.py:311
  76.3 0.9 keys.1
  77.3 1.4 copy-done.2
  78.7 5.1 %select.2 = bf16[2,8,512,128]{3,2,1,0:T(8,128)(2,1)S(1)} custom-call(s32[32,128]{1,0:T(8,128)S(1)} %get-tuple-element.11.base_ref, f32[16,2,512]{2,1,0:T(2,128)S(1)} %reshape.115.key_ref, bf16[1024,256]{1,0:T(8,128)(2,1)S(1)} %bitcast.35, bf16[16,384,128]{2,1,0:T(8,128)(2,1)S(1)} %copy-done.2), custom_call_target="tpu_custom_call" | custom-call | tf_op jit(solution)/shard_map/select/pallas_call | solution.py:340
  83.8 6.0 %em_first.2.refs_0_ = f32[264,128]{1,0:T(8,128)S(1)} custom-call(bf16[2,4096,128]{2,1,0:T(8,128)(2,1)S(1)} %bitcast.31, bf16[1024,256]{1,0:T(8,128)(2,1)S(1)} %bitcast.36, f32[256,128]{1,0:T(8,128)S(1)} %copy.28.refs_2_.refs_3_.refs_7_, f32[1,128]{1,0:T(1,128)S(1)} %reshape_reshape.3.refs_3_.refs_4_.refs_8_), custom_call_target="tpu_custom_call" | custom-call | tf_op jit(solution)/shard_map/em_first/pallas_call | solution.py:240
  89.8 7.1 %all-to-all-done.3.list_ref = bf16[16,384,128]{2,1,0:T(8,128)(2,1)} async-done(((bf16[16,384,128]{2,1,0:T(8,128)(2,1)}), bf16[16,384,128]{2,1,0:T(8,128)(2,1)}, u32[]{:S(2)}, u32[]{:S(2)}) %all-to-all-start.3) | async-done | bytes 1572896 | tf_op jit(solution)/shard_map/all_to_all | solution.py:311
  96.9 6.6 %select.3 = bf16[2,8,512,128]{3,2,1,0:T(8,128)(2,1)S(1)} custom-call(s32[32,128]{1,0:T(8,128)S(1)} %get-tuple-element.11.base_ref, f32[16,2,512]{2,1,0:T(2,128)S(1)} %reshape.115.key_ref, bf16[1024,256]{1,0:T(8,128)(2,1)S(1)} %bitcast.37, bf16[16,384,128]{2,1,0:T(8,128)(2,1)} %all-to-all-done.3.list_ref), custom_call_target="tpu_custom_call" | custom-call | tf_op jit(solution)/shard_map/select/pallas_call | solution.py:340
  103.4 6.0 %em_first.3.refs_0_ = f32[264,128]{1,0:T(8,128)S(1)} custom-call(f32[264,128]{1,0:T(8,128)S(1)} %em_first.2.refs_0_, bf16[2,4096,128]{2,1,0:T(8,128)(2,1)S(1)} %bitcast.33, bf16[1024,256]{1,0:T(8,128)(2,1)S(1)} %bitcast.38, f32[256,128]{1,0:T(8,128)S(1)} %copy.28.refs_2_.refs_3_.refs_7_, f32[1,128]{1,0:T(1,128)S(1)} %reshape_reshape.3.refs_3_.refs_4_.refs_8_), custom_call_target="tpu_custom_call" | custom-call | tf_op jit(solution)/shard_map/em_first/pallas_call | solution.py:240
  109.5 4.3 %collective-permute-start.1 = (f32[264,128]{1,0:T(8,128)S(1)}, f32[264,128]{1,0:T(8,128)S(1)}, u32[]{:S(2)}, u32[]{:S(2)}) collective-permute-start(f32[264,128]{1,0:T(8,128)S(1)} %em_first.3.refs_0_), channel_id=1, source_target_pairs={{0,16},{8,24},{16,0},{24,8},{1,17},{9,25},{17,1},{25,9},{2,18},{10... | collective-permute-start | bytes 405512 | tf_op jit(solution)/shard_map/ppermute | solution.py:277
  113.8 1.4 collective-permute-done.refs_1_
  115.2 2.6 %collective-permute-done.1.refs_2_ = f32[264,128]{1,0:T(8,128)S(1)} collective-permute-done((f32[264,128]{1,0:T(8,128)S(1)}, f32[264,128]{1,0:T(8,128)S(1)}, u32[]{:S(2)}, u32[]{:S(2)}) %collective-permute-start.1) | collective-permute-done | bytes 135200 | tf_op jit(solution)/shard_map/ppermute | solution.py:277
  117.7 1.4 collective-permute-done.2.refs_3_
  119.1 13.5 %em_last.1 = (f32[264,128]{1,0:T(8,128)S(1)}, f32[256,128]{1,0:T(8,128)S(1)}, f32[8,8,128]{2,1,0:T(8,128)S(1)}) custom-call(f32[264,128]{1,0:T(8,128)S(1)} %em_first.3.refs_0_, f32[264,128]{1,0:T(8,128)S(1)} %collective-permute-done.refs_1_, f32[264,128]{1,0:T(8,128)S(1)} %collective-permute-done.1.refs_2_, f32[264,128]{1,0:T(8,128)S(1)} %collective-permute-done.2.refs_3_, ...), custom_call_target="tpu_custom_call" | custom-call | tf_op jit(solution)/shard_map/em_last/pallas_call | solution.py:240
  132.6 0.7 copy-done.7
  133.3 0.6 collective-permute-start.3
  133.9 2.6 %collective-permute-start.4 = (f32[264,128]{1,0:T(8,128)S(1)}, f32[264,128]{1,0:T(8,128)S(1)}, u32[]{:S(2)}, u32[]{:S(2)}) collective-permute-start(f32[264,128]{1,0:T(8,128)S(1)} %get-tuple-element.15.p0), channel_id=1, source_target_pairs={{0,16},{8,24},{16,0},{24,8},{1,17},{9,25},{17,1},{25,9},{2,18},{10... | collective-permute-start | bytes 405512 | tf_op jit(solution)/shard_map/ppermute | solution.py:277
  136.5 1.7 %collective-permute-start.5 = (f32[264,128]{1,0:T(8,128)S(1)}, f32[264,128]{1,0:T(8,128)S(1)}, u32[]{:S(2)}, u32[]{:S(2)}) collective-permute-start(f32[264,128]{1,0:T(8,128)S(1)} %get-tuple-element.15.p0), channel_id=1, source_target_pairs={{0,24},{8,0},{16,8},{24,16},{1,25},{9,1},{17,9},{25,17},{2,26},{10... | collective-permute-start | bytes 405512 | tf_op jit(solution)/shard_map/ppermute | solution.py:277
  138.2 9.6 %all_to_all.25.err_ref = f32[8,8,128]{2,1,0:T(8,128)} all-to-all(f32[8,8,128]{2,1,0:T(8,128)S(1)} %get-tuple-element.17), channel_id=1, replica_groups=mesh['z'=4,'y'=4,'sub'=8] {'sub'}, dimensions={0} | all-to-all | bytes 65536 | tf_op jit(solution)/shard_map/all_to_all | solution.py:364
  147.9 0.6 copy-done.11
  148.6 2.0 %update.1.x0 = f32[136,256]{1,0:T(8,128)} custom-call(f32[264,128]{1,0:T(8,128)} %copy-done.6, f32[264,128]{1,0:T(8,128)} %copy-done.11, f32[264,128]{1,0:T(8,128)} %copy-done.12, f32[264,128]{1,0:T(8,128)} %copy-done.13, f32[256,128]{1,0:T(8,128)} %copy-done.7, f32[8,8,128]{2,1,0:T(8,128)} %all_to_all.25.err_ref), custom_call_target="tpu_custom_call" | custom-call | tf_op jit(solution)/shard_map/update/pallas_call | solution.py:365
  150.6 0.9 collective-permute-start.6
  151.5 1.9 %collective-permute-start.7 = (f32[136,256]{1,0:T(8,128)}, f32[136,256]{1,0:T(8,128)S(1)}, u32[]{:S(2)}, u32[]{:S(2)}) collective-permute-start(f32[136,256]{1,0:T(8,128)} %update.1.x0), channel_id=1, source_target_pairs={{0,64},{32,96},{64,0},{96,32},{1,65},{33,97},{65,1},{97,33},{2,66}... | collective-permute-start | bytes 417800 | tf_op jit(solution)/shard_map/ppermute | solution.py:277
  153.5 1.3 collective-permute-start.8
  154.7 0.6 multiply_bitcast_fusion.keep_ref
  155.3 5.1 %collective-permute-done.6.x1 = f32[136,256]{1,0:T(8,128)S(1)} collective-permute-done((f32[136,256]{1,0:T(8,128)}, f32[136,256]{1,0:T(8,128)S(1)}, u32[]{:S(2)}, u32[]{:S(2)}) %collective-permute-start.6) | collective-permute-done | bytes 139296 | tf_op jit(solution)/shard_map/ppermute | solution.py:277
  160.4 0.6 collective-permute-done.8.x3
  161.1 0.5 copy-done.10
  161.6 1.9 %assemble.1 = (f32[4,128,256]{2,1,0:T(8,128)}, f32[8,32]{1,0:T(8,128)}) custom-call(s32[1]{0:T(128)} %bitcast.z_ref, f32[136,256]{1,0:T(8,128)} %update.1.x0, f32[136,256]{1,0:T(8,128)} %copy-done.8, f32[136,256]{1,0:T(8,128)} %copy-done.9, f32[136,256]{1,0:T(8,128)} %copy-done.10, f32[8,32]{1,0:T(8,128)} %multiply_bitcast_fusion.keep_ref), custom_call_target="tpu_custom_call" | custom-call | tf_op jit(solution)/shard_map/assemble/pallas_call | solution.py:373
  (56 shorter events, 1.8 us)
Async XLA Ops:
  0.6 75.3 %copy-start = (f32[8,256,64]{1,2,0:T(8,128)S(1)}, f32[8,256,64]{1,2,0:T(8,128)}, u32[]{:S(2)}) copy-start(f32[8,256,64]{1,2,0:T(8,128)} %param.14) | copy-start | bytes 1572868
  2.9 19.5 %all-to-all-start = ((s32[128,2,128]{2,1,0:T(2,128)}), s32[128,2,128]{2,1,0:T(2,128)S(1)}, u32[]{:S(2)}, u32[]{:S(2)}) async-start(s32[128,2,128]{2,1,0:T(2,128)} %broadcast_in_dim.49), calls=%async_computation | async-start | bytes 262144 | tf_op jit(solution)/shard_map/all_to_all | solution.py:288
  22.4 16.3 %all-to-all-start.1 = ((bf16[32,32,256]{2,1,0:T(8,128)(2,1)}), bf16[32,32,256]{2,1,0:T(8,128)(2,1)S(1)}, u32[]{:S(2)}, u32[]{:S(2)}) async-start(bf16[32,32,256]{2,1,0:T(8,128)(2,1)} %pad_maximum_fusion), calls=%async_computation.1 | async-start | bytes 1048576 | tf_op jit(solution)/shard_map/all_to_all | solution.py:327
  37.5 1.1 copy-start.4
  38.7 28.6 %all-to-all-start.2 = ((bf16[16,384,128]{2,1,0:T(8,128)(2,1)}), bf16[16,384,128]{2,1,0:T(8,128)(2,1)S(1)}, u32[]{:S(2)}, u32[]{:S(2)}) async-start(bf16[16,384,128]{2,1,0:T(8,128)(2,1)} %bitcast.41), calls=%async_computation.2 | async-start | bytes 3145728 | tf_op jit(solution)/shard_map/all_to_all | solution.py:311
  55.4 1.4 copy-start.5
  57.1 1.2 copy-start.3
  67.3 1.2 copy-start.1
  67.3 8.8 %copy-start.15 = (f32[8]{0:T(128)S(1)}, f32[8]{0:T(128)}, u32[]{:S(2)}) copy-start(f32[8]{0:T(128)} %param.15) | copy-start | bytes 100
  68.4 28.4 %all-to-all-start.3 = ((bf16[16,384,128]{2,1,0:T(8,128)(2,1)}), bf16[16,384,128]{2,1,0:T(8,128)(2,1)}, u32[]{:S(2)}, u32[]{:S(2)}) async-start(bf16[16,384,128]{2,1,0:T(8,128)(2,1)} %bitcast.40), calls=%async_computation.3 | async-start | bytes 3145728 | tf_op jit(solution)/shard_map/all_to_all | solution.py:311
  77.2 1.4 copy-start.2
  109.4 45.3 %copy-start.14 = (s32[32,8]{0,1:T(8,128)S(1)}, s32[32,8]{0,1:T(8,128)}, u32[]{:S(2)}) copy-start(s32[32,8]{0,1:T(8,128)} %param.11) | copy-start | bytes 3076
  109.4 5.7 %collective-permute-start = (f32[264,128]{1,0:T(8,128)S(1)}, f32[264,128]{1,0:T(8,128)S(1)}, u32[]{:S(2)}, u32[]{:S(2)}) collective-permute-start(f32[264,128]{1,0:T(8,128)S(1)} %em_first.3.refs_0_), channel_id=1, source_target_pairs={{0,8},{8,16},{16,24},{24,0},{1,9},{9,17},{17,25},{25,1},{2,10},{10... | collective-permute-start | bytes 405512 | tf_op jit(solution)/shard_map/ppermute | solution.py:277
  109.5 8.2 %collective-permute-start.1 = (f32[264,128]{1,0:T(8,128)S(1)}, f32[264,128]{1,0:T(8,128)S(1)}, u32[]{:S(2)}, u32[]{:S(2)}) collective-permute-start(f32[264,128]{1,0:T(8,128)S(1)} %em_first.3.refs_0_), channel_id=1, source_target_pairs={{0,16},{8,24},{16,0},{24,8},{1,17},{9,25},{17,1},{25,9},{2,18},{10... | collective-permute-start | bytes 405512 | tf_op jit(solution)/shard_map/ppermute | solution.py:277
  113.8 5.4 %collective-permute-start.2 = (f32[264,128]{1,0:T(8,128)S(1)}, f32[264,128]{1,0:T(8,128)S(1)}, u32[]{:S(2)}, u32[]{:S(2)}) collective-permute-start(f32[264,128]{1,0:T(8,128)S(1)} %em_first.3.refs_0_), channel_id=1, source_target_pairs={{0,24},{8,0},{16,8},{24,16},{1,25},{9,1},{17,9},{25,17},{2,26},{10... | collective-permute-start | bytes 405512 | tf_op jit(solution)/shard_map/ppermute | solution.py:277
  132.6 0.7 copy-start.7
  133.3 14.6 %copy-start.6 = (f32[264,128]{1,0:T(8,128)}, f32[264,128]{1,0:T(8,128)S(1)}, u32[]{:S(2)}) copy-start(f32[264,128]{1,0:T(8,128)S(1)} %get-tuple-element.15.p0) | copy-start | bytes 405508
  133.3 14.6 %collective-permute-start.3 = (f32[264,128]{1,0:T(8,128)S(1)}, f32[264,128]{1,0:T(8,128)S(1)}, u32[]{:S(2)}, u32[]{:S(2)}) collective-permute-start(f32[264,128]{1,0:T(8,128)S(1)} %get-tuple-element.15.p0), channel_id=1, source_target_pairs={{0,8},{8,16},{16,24},{24,0},{1,9},{9,17},{17,25},{25,1},{2,10},{10... | collective-permute-start | bytes 405512 | tf_op jit(solution)/shard_map/ppermute | solution.py:277
  133.9 14.0 %collective-permute-start.4 = (f32[264,128]{1,0:T(8,128)S(1)}, f32[264,128]{1,0:T(8,128)S(1)}, u32[]{:S(2)}, u32[]{:S(2)}) collective-permute-start(f32[264,128]{1,0:T(8,128)S(1)} %get-tuple-element.15.p0), channel_id=1, source_target_pairs={{0,16},{8,24},{16,0},{24,8},{1,17},{9,25},{17,1},{25,9},{2,18},{10... | collective-permute-start | bytes 405512 | tf_op jit(solution)/shard_map/ppermute | solution.py:277
  136.5 11.4 %collective-permute-start.5 = (f32[264,128]{1,0:T(8,128)S(1)}, f32[264,128]{1,0:T(8,128)S(1)}, u32[]{:S(2)}, u32[]{:S(2)}) collective-permute-start(f32[264,128]{1,0:T(8,128)S(1)} %get-tuple-element.15.p0), channel_id=1, source_target_pairs={{0,24},{8,0},{16,8},{24,16},{1,25},{9,1},{17,9},{25,17},{2,26},{10... | collective-permute-start | bytes 405512 | tf_op jit(solution)/shard_map/ppermute | solution.py:277
  147.9 0.6 copy-start.11
  147.9 0.7 copy-start.12
  147.9 0.7 copy-start.13
  150.6 9.8 %collective-permute-start.6 = (f32[136,256]{1,0:T(8,128)}, f32[136,256]{1,0:T(8,128)S(1)}, u32[]{:S(2)}, u32[]{:S(2)}) collective-permute-start(f32[136,256]{1,0:T(8,128)} %update.1.x0), channel_id=1, source_target_pairs={{0,32},{32,64},{64,96},{96,0},{1,33},{33,65},{65,97},{97,1},{2,34}... | collective-permute-start | bytes 417800 | tf_op jit(solution)/shard_map/ppermute | solution.py:277
  151.5 8.9 %collective-permute-start.7 = (f32[136,256]{1,0:T(8,128)}, f32[136,256]{1,0:T(8,128)S(1)}, u32[]{:S(2)}, u32[]{:S(2)}) collective-permute-start(f32[136,256]{1,0:T(8,128)} %update.1.x0), channel_id=1, source_target_pairs={{0,64},{32,96},{64,0},{96,32},{1,65},{33,97},{65,1},{97,33},{2,66}... | collective-permute-start | bytes 417800 | tf_op jit(solution)/shard_map/ppermute | solution.py:277
  153.5 7.5 %collective-permute-start.8 = (f32[136,256]{1,0:T(8,128)}, f32[136,256]{1,0:T(8,128)S(1)}, u32[]{:S(2)}, u32[]{:S(2)}) collective-permute-start(f32[136,256]{1,0:T(8,128)} %update.1.x0), channel_id=1, source_target_pairs={{0,96},{32,0},{64,32},{96,64},{1,97},{33,1},{65,33},{97,65},{2,98}... | collective-permute-start | bytes 417800 | tf_op jit(solution)/shard_map/ppermute | solution.py:277
  160.4 0.6 copy-start.8
  160.4 0.7 copy-start.9
  161.0 0.7 copy-start.10

commit v4 on v3

--- a/solution.py
+++ b/solution.py
@@ -31,7 +31,7 @@
     return jnp.where(cond, 1.0, 0.0).astype(BF16)
 
 
-def params(mib=48):
+def params(mib=8):
     return pltpu.CompilerParams(vmem_limit_bytes=mib << 20)
 
 
@@ -44,6 +44,12 @@
     y = lax.shift_right_logical(d, 3) & 3
     q = lax.shift_right_logical(d, 5) * 8 + (d & 7)
     return y, q
+
+
+def send_kernel(owner_ref, local_ref, mask_ref, out_ref):
+    posting = jnp.where(mask_ref[...] > 0, owner_ref[...] * 8192 + local_ref[...], -1)
+    rows = [jnp.concatenate([posting[4 * h + t : 4 * h + t + 1] for t in range(4)], 1) for h in range(2)]
+    out_ref[...] = jnp.broadcast_to(jnp.concatenate(rows, 0)[None], (128, 2, 128))
 
 
 def list_kernel(me_ref, ids_ref, first_ref, second_ref):
@@ -107,33 +113,46 @@
     key_ref[...] = jnp.where((col & 31).astype(F32) >= gap, col.astype(F32) - gap, -1.0)
 
 
-def split_kernel(rows_ref, out_ref):
+def split_kernel(rows_ref, out_ref, held_ref, sem):
+    copies = []
     for c in range(4):
-        out_ref[c] = rows_ref[:, 128 * c : 128 * c + 128]
+        held_ref[c] = rows_ref[:, 128 * c : 128 * c + 128]
+        copies.append(pltpu.make_async_copy(held_ref.at[c], out_ref.at[c], sem.at[c]))
+        copies[c].start()
+    for copy in copies:
+        copy.wait()
 
 
 def select_kernel(half, base_ref, key_ref, rows_ref, list_ref, out_ref):
-    g = pl.program_id(0) + 8 * half
-    meta = rows_ref[:, 128:256].astype(F32)
-    v = rows_ref[:, 0:128].astype(F32)
-    v_roll = pltpu.roll(v, 64, 1)
     left = iota((32, 128), 1) < 64
-    for b in range(2):
+
+    def block(i):
+        b = 16 * half + i
+        rows = rows_ref[pl.ds(pl.multiple_of(32 * b, 32), 32), :].astype(F32)
+        v, meta = rows[:, 0:128], rows[:, 128:256]
+        v_roll = pltpu.roll(v, 64, 1)
         parts = []
         for p in range(16):
-            at = pl.multiple_of(base_ref[2 * g + b, p], 8)
+            at = pl.multiple_of(base_ref[b, p], 8)
             parts.append(list_ref[p, pl.ds(at, WINDOW), :])
-        key = key_ref[0, b : b + 1]
-        own = slice(32 * b, 32 * b + 32)
+        key = key_ref[pl.ds(b, 1), :]
         hot = []
         for t in range(8):
-            want = meta[own, t : t + 1] * float(WINDOW) + meta[own, 8 + t : 9 + t]
+            want = meta[:, t : t + 1] * float(WINDOW) + meta[:, 8 + t : 9 + t]
             hot.append(ones_where(want == key))
         got = dot(jnp.concatenate(hot, 0), jnp.concatenate(parts, 0))
+        own = pl.ds(pl.multiple_of(32 * i, 32), 32)
         for t in range(8):
             c = got[32 * t : 32 * t + 32]
-            out_ref[0, t, own] = jnp.where(left, v[own], pltpu.roll(c, 64, 1)).astype(BF16)
-            out_ref[1, t, own] = jnp.where(left, v_roll[own], c).astype(BF16)
+            out_ref[0, t, own] = jnp.where(left, v, pltpu.roll(c, 64, 1)).astype(BF16)
+            out_ref[1, t, own] = jnp.where(left, v_roll, c).astype(BF16)
+
+    def pair(i, carry):
+        block(2 * i)
+        block(2 * i + 1)
+        return carry
+
+    lax.fori_loop(0, 8, pair, 0)
 
 
 def combine(parts, words):
@@ -248,7 +267,7 @@
             pltpu.VMEM((2, 256, 256), F32),
             pltpu.VMEM((8, 1024), F32),
         ],
-        compiler_params=params(),
+        compiler_params=params(24),
         name="em_last" if last else "em_first",
     )(*args)
 
@@ -284,10 +303,14 @@
     valid = mask > 0
     owned = jnp.where(valid, owner, -1)
 
-    posting = jnp.where(valid, owner * 8192 + local, -1).T.reshape(1, 2, 128)
-    ids = lax.all_to_all(
-        jnp.broadcast_to(posting, (128, 2, 128)), ("z", "y", "sub"), 0, 0, tiled=True
-    ).reshape(256, 128)
+    posting = pl.pallas_call(
+        send_kernel,
+        out_shape=jax.ShapeDtypeStruct((128, 2, 128), jnp.int32),
+        in_specs=[VMEM] * 3,
+        out_specs=VMEM,
+        name="send",
+    )(owner.T, local.T, mask.T)
+    ids = lax.all_to_all(posting, ("z", "y", "sub"), 0, 0, tiled=True).reshape(256, 128)
 
     wanted = pl.pallas_call(
         list_kernel,
@@ -304,7 +327,8 @@
             split_kernel,
             out_shape=jax.ShapeDtypeStruct((4, 4 * CAP, 128), BF16),
             in_specs=[VMEM],
-            out_specs=VMEM,
+            out_specs=pl.BlockSpec(memory_space=pltpu.HBM),
+            scratch_shapes=[pltpu.VMEM((4, 4 * CAP, 128), BF16), pltpu.SemaphoreType.DMA((4,))],
             compiler_params=params(),
             name="split",
         )(found)
@@ -334,23 +358,14 @@
         compiler_params=params(),
         name="keys",
     )(y1, ids)
-    keys = keys.reshape(16, 2, 512)
 
     def select(half):
         return pl.pallas_call(
             functools.partial(select_kernel, half),
             out_shape=jax.ShapeDtypeStruct((2, 8, 512, 128), BF16),
-            grid_spec=pltpu.PrefetchScalarGridSpec(
-                num_scalar_prefetch=1,
-                grid=(8,),
-                in_specs=[
-                    pl.BlockSpec((1, 2, 512), lambda g, b: (g + 8 * half, 0, 0)),
-                    pl.BlockSpec((64, 256), lambda g, b: (g + 8 * half, 0)),
-                    pl.BlockSpec((16, CAP, 128), lambda g, b: (0, 0, 0)),
-                ],
-                out_specs=pl.BlockSpec((2, 8, 64, 128), lambda g, b: (0, 0, g, 0)),
-            ),
-            compiler_params=params(),
+            in_specs=[SMEM] + [VMEM] * 3,
+            out_specs=VMEM,
+            compiler_params=params(12),
             name="select",
         )(base, keys, rows, lists[half]).reshape(2, 4096, 128)
 
@@ -367,6 +382,7 @@
         out_shape=jax.ShapeDtypeStruct((136, 256), F32),
         in_specs=[VMEM] * 6,
         out_specs=VMEM,
+        compiler_params=params(),
         name="update",
     )(*shifts(part, "y"), words, error)
     keep = mask.T.astype(F32) / vectors.shape[1]
@@ -375,6 +391,7 @@
         out_shape=[jax.ShapeDtypeStruct((4, 128, 256), F32), jax.ShapeDtypeStruct((8, 32), F32)],
         in_specs=[SMEM] + [VMEM] * 5,
         out_specs=[VMEM] * 2,
+        compiler_params=params(),
         name="assemble",
     )(z1, *shifts(turned, "z"), keep)
     return trained.reshape(8, 64, 256).transpose(0, 2, 1), error.T

time: 164 us -> 158 us (0.963)
  local copies, waits for them, and re-layouts: 30.4 us -> 27.5 us
    unnamed x34 -> x18, local copies, waits for them, and re-layouts: 8.35 us -> 6.3 us
    pallas_call x1, Pallas kernels: 2.04 us -> 0.23 us  [per_device(): pl.pallas_call(update_kernel, out_shape=jax.ShapeDtypeStruct((136, 256),...]
  transfers between devices with their start and end apart: 13 -> 13, of which waited for: 8 -> 8; matrix products, arithmetic and copies ran while one was open for 15% -> 15% of each run, Pallas kernels for 9% -> 10%
where the time goes in v4:
time: 158 us; the launch traced here: 157 us
  Pallas kernels  43.1 us (27%)
  starting transfers between devices  42.2 us (27%)
  waiting for transfers between devices  31.7 us (20%)
  local copies, waits for them, and re-layouts  27.5 us (17%)
  blocking collectives  9.5 us (6%)
  other arithmetic  2.49 us (2%)
    pallas_call x3, Pallas kernels, em(): pl.pallas_call(functools.partial(em_kernel, halves, carried, last), out_s...  25.4 us
    gather x2, local copies, waits for them, and re-layouts, fetch(): found = centroids.at[want.reshape(4 * CAP)].get(mode='promise_in_bounds')  19.3 us
    all_to_all x2, waiting for transfers between devices, fetch(): lax.all_to_all(found.reshape(16, CAP, 128), ('z', 'y'), 0, 0, tiled=True)  15.5 us
    all_to_all x2, starting transfers between devices, fetch(): lax.all_to_all(found.reshape(16, CAP, 128), ('z', 'y'), 0, 0, tiled=True)  14.3 us
    ppermute x9, starting transfers between devices, shifts(): return [x] + [lax.ppermute(x, axis, turn(d)) for d in (1, 2, 3)]  13.5 us
    ppermute x9, waiting for transfers between devices, shifts(): return [x] + [lax.ppermute(x, axis, turn(d)) for d in (1, 2, 3)]  11.4 us
    all_to_all x1, starting transfers between devices, per_device(): lax.all_to_all(posting, ('z', 'y', 'sub'), 0, 0, tiled=True)  10.4 us
    pallas_call x2, Pallas kernels, select(): pl.pallas_call(functools.partial(select_kernel, half), out_shape=jax.Shap...  10.4 us
  transfers between devices with their start and end apart: 13, of which 8 were waited for; matrix products, arithmetic and copies ran while one was open for 15% of the time, Pallas kernels for 10%

profile of v4, /device:TPU:8, one launch (start us, length us, event | category | flops | bytes accessed | tf_op | source)
XLA Modules:
  0.0 157.5 jit_solution(8956741950896078293)
XLA Ops:
  0.6 1.6 send.1
  2.2 10.4 %all-to-all-start = ((s32[128,2,128]{2,1,0:T(2,128)}), s32[128,2,128]{2,1,0:T(2,128)S(1)}, u32[]{:S(2)}, u32[]{:S(2)}) async-start(s32[128,2,128]{2,1,0:T(2,128)} %send.1), calls=%async_computation | async-start | bytes 262144 | tf_op jit(solution)/shard_map/all_to_all | solution.py:313
  12.7 0.7 fusion.10
  13.4 0.2 fusion.1
  13.6 0.1 copy.26
  13.8 0.7 convert_multiply_fusion.1
  14.5 0.1 copy.27
  14.8 1.1 reshape.110
  15.9 0.1 copy.24
  16.0 0.9 pad_maximum_fusion
  16.9 4.8 %all-to-all-done = s32[128,2,128]{2,1,0:T(2,128)S(1)} async-done(((s32[128,2,128]{2,1,0:T(2,128)}), s32[128,2,128]{2,1,0:T(2,128)S(1)}, u32[]{:S(2)}, u32[]{:S(2)}) %all-to-all-start) | async-done | bytes 131104 | tf_op jit(solution)/shard_map/all_to_all | solution.py:313
  21.7 3.9 %all-to-all-start.1 = ((bf16[32,32,256]{2,1,0:T(8,128)(2,1)}), bf16[32,32,256]{2,1,0:T(8,128)(2,1)S(1)}, u32[]{:S(2)}, u32[]{:S(2)}) async-start(bf16[32,32,256]{2,1,0:T(8,128)(2,1)} %pad_maximum_fusion), calls=%async_computation.1 | async-start | bytes 1048576 | tf_op jit(solution)/shard_map/all_to_all | solution.py:351
  25.6 1.6 lists.1
  27.2 9.3 %gather_fusion = bf16[1536,512]{1,0:T(8,128)(2,1)S(1)} fusion(bf16[8192,512]{1,0:T(8,128)(2,1)} %param.13, s32[2048]{0:T(1024)S(1)} %pad_clamp_fusion.1), kind=kCustom, calls=%fused_computation | custom fusion | bytes 3151872 | tf_op jit(solution)/shard_map/gather | solution.py:325
  36.6 1.1 split.2
  37.7 1.1 copy-done.4
  38.8 6.8 %all-to-all-start.2 = ((bf16[16,384,128]{2,1,0:T(8,128)(2,1)}), bf16[16,384,128]{2,1,0:T(8,128)(2,1)S(1)}, u32[]{:S(2)}, u32[]{:S(2)}) async-start(bf16[16,384,128]{2,1,0:T(8,128)(2,1)} %bitcast.41), calls=%async_computation.2 | async-start | bytes 3145728 | tf_op jit(solution)/shard_map/all_to_all | solution.py:335
  45.6 9.9 %gather_fusion.1 = bf16[1536,512]{1,0:T(8,128)(2,1)} fusion(bf16[8192,512]{1,0:T(8,128)(2,1)} %param.13, s32[2048]{0:T(1024)S(1)} %pad_clamp_fusion), kind=kCustom, calls=%fused_computation.1 | custom fusion | bytes 3151872 | tf_op jit(solution)/shard_map/gather | solution.py:325
  55.6 1.4 copy-done.5
  57.0 1.1 split.3
  58.0 1.2 copy-done.3
  59.2 8.2 %all-to-all-done.2.list_ref = bf16[16,384,128]{2,1,0:T(8,128)(2,1)S(1)} async-done(((bf16[16,384,128]{2,1,0:T(8,128)(2,1)}), bf16[16,384,128]{2,1,0:T(8,128)(2,1)S(1)}, u32[]{:S(2)}, u32[]{:S(2)}) %all-to-all-start.2) | async-done | bytes 1572896 | tf_op jit(solution)/shard_map/all_to_all | solution.py:335
  67.4 1.2 copy-done.1
  68.5 7.5 %all-to-all-start.3 = ((bf16[16,384,128]{2,1,0:T(8,128)(2,1)}), bf16[16,384,128]{2,1,0:T(8,128)(2,1)}, u32[]{:S(2)}, u32[]{:S(2)}) async-start(bf16[16,384,128]{2,1,0:T(8,128)(2,1)} %bitcast.40), calls=%async_computation.3 | async-start | bytes 3145728 | tf_op jit(solution)/shard_map/all_to_all | solution.py:335
  76.4 0.9 keys.1
  77.3 1.4 copy-done.2
  78.7 4.9 %select.2 = bf16[2,8,512,128]{3,2,1,0:T(8,128)(2,1)S(1)} custom-call(s32[32,128]{1,0:T(8,128)S(1)} %get-tuple-element.11.base_ref, f32[32,512]{1,0:T(8,128)S(1)} %get-tuple-element.12.key_ref, bf16[1024,256]{1,0:T(8,128)(2,1)S(1)} %bitcast.35, bf16[16,384,128]{2,1,0:T(8,128)(2,1)S(1)} %copy-done.2), custom_call_target="tpu_custom_call" | custom-call | tf_op jit(solution)/shard_map/select/pallas_call | solution.py:363
  83.6 6.0 %em_first.2.refs_0_ = f32[264,128]{1,0:T(8,128)S(1)} custom-call(bf16[2,4096,128]{2,1,0:T(8,128)(2,1)S(1)} %bitcast.31, bf16[1024,256]{1,0:T(8,128)(2,1)S(1)} %bitcast.36, f32[256,128]{1,0:T(8,128)S(1)} %copy.28.refs_2_.refs_3_.refs_7_, f32[1,128]{1,0:T(1,128)S(1)} %reshape_reshape.3.refs_3_.refs_4_.refs_8_), custom_call_target="tpu_custom_call" | custom-call | tf_op jit(solution)/shard_map/em_first/pallas_call | solution.py:259
  89.6 7.3 %all-to-all-done.3.list_ref = bf16[16,384,128]{2,1,0:T(8,128)(2,1)} async-done(((bf16[16,384,128]{2,1,0:T(8,128)(2,1)}), bf16[16,384,128]{2,1,0:T(8,128)(2,1)}, u32[]{:S(2)}, u32[]{:S(2)}) %all-to-all-start.3) | async-done | bytes 1572896 | tf_op jit(solution)/shard_map/all_to_all | solution.py:335
  97.0 5.5 %select.3 = bf16[2,8,512,128]{3,2,1,0:T(8,128)(2,1)S(1)} custom-call(s32[32,128]{1,0:T(8,128)S(1)} %get-tuple-element.11.base_ref, f32[32,512]{1,0:T(8,128)S(1)} %get-tuple-element.12.key_ref, bf16[1024,256]{1,0:T(8,128)(2,1)S(1)} %bitcast.37, bf16[16,384,128]{2,1,0:T(8,128)(2,1)} %all-to-all-done.3.list_ref), custom_call_target="tpu_custom_call" | custom-call | tf_op jit(solution)/shard_map/select/pallas_call | solution.py:363
  102.5 6.0 %em_first.3.refs_0_ = f32[264,128]{1,0:T(8,128)S(1)} custom-call(f32[264,128]{1,0:T(8,128)S(1)} %em_first.2.refs_0_, bf16[2,4096,128]{2,1,0:T(8,128)(2,1)S(1)} %bitcast.33, bf16[1024,256]{1,0:T(8,128)(2,1)S(1)} %bitcast.38, f32[256,128]{1,0:T(8,128)S(1)} %copy.28.refs_2_.refs_3_.refs_7_, f32[1,128]{1,0:T(1,128)S(1)} %reshape_reshape.3.refs_3_.refs_4_.refs_8_), custom_call_target="tpu_custom_call" | custom-call | tf_op jit(solution)/shard_map/em_first/pallas_call | solution.py:259
  108.5 0.1 collective-permute-start
  108.6 4.3 %collective-permute-start.1 = (f32[264,128]{1,0:T(8,128)S(1)}, f32[264,128]{1,0:T(8,128)S(1)}, u32[]{:S(2)}, u32[]{:S(2)}) collective-permute-start(f32[264,128]{1,0:T(8,128)S(1)} %em_first.3.refs_0_), channel_id=1, source_target_pairs={{0,16},{8,24},{16,0},{24,8},{1,17},{9,25},{17,1},{25,9},{2,18},{10... | collective-permute-start | bytes 405512 | tf_op jit(solution)/shard_map/ppermute | solution.py:296
  112.9 1.4 collective-permute-done.refs_1_
  114.2 2.6 %collective-permute-done.1.refs_2_ = f32[264,128]{1,0:T(8,128)S(1)} collective-permute-done((f32[264,128]{1,0:T(8,128)S(1)}, f32[264,128]{1,0:T(8,128)S(1)}, u32[]{:S(2)}, u32[]{:S(2)}) %collective-permute-start.1) | collective-permute-done | bytes 135200 | tf_op jit(solution)/shard_map/ppermute | solution.py:296
  116.8 1.4 collective-permute-done.2.refs_3_
  118.2 13.5 %em_last.1 = (f32[264,128]{1,0:T(8,128)S(1)}, f32[256,128]{1,0:T(8,128)S(1)}, f32[8,8,128]{2,1,0:T(8,128)S(1)}) custom-call(f32[264,128]{1,0:T(8,128)S(1)} %em_first.3.refs_0_, f32[264,128]{1,0:T(8,128)S(1)} %collective-permute-done.refs_1_, f32[264,128]{1,0:T(8,128)S(1)} %collective-permute-done.1.refs_2_, f32[264,128]{1,0:T(8,128)S(1)} %collective-permute-done.2.refs_3_, ...), custom_call_target="tpu_custom_call" | custom-call | tf_op jit(solution)/shard_map/em_last/pallas_call | solution.py:259
  131.7 0.6 collective-permute-start.3
  132.3 2.6 %collective-permute-start.4 = (f32[264,128]{1,0:T(8,128)S(1)}, f32[264,128]{1,0:T(8,128)S(1)}, u32[]{:S(2)}, u32[]{:S(2)}) collective-permute-start(f32[264,128]{1,0:T(8,128)S(1)} %get-tuple-element.15.p0), channel_id=1, source_target_pairs={{0,16},{8,24},{16,0},{24,8},{1,17},{9,25},{17,1},{25,9},{2,18},{10... | collective-permute-start | bytes 405512 | tf_op jit(solution)/shard_map/ppermute | solution.py:296
  135.0 1.7 %collective-permute-start.5 = (f32[264,128]{1,0:T(8,128)S(1)}, f32[264,128]{1,0:T(8,128)S(1)}, u32[]{:S(2)}, u32[]{:S(2)}) collective-permute-start(f32[264,128]{1,0:T(8,128)S(1)} %get-tuple-element.15.p0), channel_id=1, source_target_pairs={{0,24},{8,0},{16,8},{24,16},{1,25},{9,1},{17,9},{25,17},{2,26},{10... | collective-permute-start | bytes 405512 | tf_op jit(solution)/shard_map/ppermute | solution.py:296
  136.7 9.5 %all_to_all.25.err_ref = f32[8,8,128]{2,1,0:T(8,128)S(1)} all-to-all(f32[8,8,128]{2,1,0:T(8,128)S(1)} %get-tuple-element.17), channel_id=1, replica_groups=mesh['z'=4,'y'=4,'sub'=8] {'sub'}, dimensions={0} | all-to-all | bytes 65536 | tf_op jit(solution)/shard_map/all_to_all | solution.py:379
  146.2 0.2 update.1.x0
  146.4 1.0 collective-permute-start.6
  147.4 1.9 %collective-permute-start.7 = (f32[136,256]{1,0:T(8,128)S(1)}, f32[136,256]{1,0:T(8,128)S(1)}, u32[]{:S(2)}, u32[]{:S(2)}) collective-permute-start(f32[136,256]{1,0:T(8,128)S(1)} %update.1.x0), channel_id=1, source_target_pairs={{0,64},{32,96},{64,0},{96,32},{1,65},{33,97},{65,1},{97,33},{2,66}... | collective-permute-start | bytes 417800 | tf_op jit(solution)/shard_map/ppermute | solution.py:296
  149.3 1.3 collective-permute-start.8
  150.6 5.4 %collective-permute-done.6.x1 = f32[136,256]{1,0:T(8,128)S(1)} collective-permute-done((f32[136,256]{1,0:T(8,128)S(1)}, f32[136,256]{1,0:T(8,128)S(1)}, u32[]{:S(2)}, u32[]{:S(2)}) %collective-permute-start.6) | collective-permute-done | bytes 139296 | tf_op jit(solution)/shard_map/ppermute | solution.py:296
  156.1 0.6 collective-permute-done.8.x3
  156.6 0.8 assemble.1
  (37 shorter events, 0.8 us)
Async XLA Ops:
  0.6 75.4 %copy-start = (f32[8,256,64]{1,2,0:T(8,128)S(1)}, f32[8,256,64]{1,2,0:T(8,128)}, u32[]{:S(2)}) copy-start(f32[8,256,64]{1,2,0:T(8,128)} %param.14) | copy-start | bytes 1572868
  2.2 19.5 %all-to-all-start = ((s32[128,2,128]{2,1,0:T(2,128)}), s32[128,2,128]{2,1,0:T(2,128)S(1)}, u32[]{:S(2)}, u32[]{:S(2)}) async-start(s32[128,2,128]{2,1,0:T(2,128)} %send.1), calls=%async_computation | async-start | bytes 262144 | tf_op jit(solution)/shard_map/all_to_all | solution.py:313
  21.7 17.1 %all-to-all-start.1 = ((bf16[32,32,256]{2,1,0:T(8,128)(2,1)}), bf16[32,32,256]{2,1,0:T(8,128)(2,1)S(1)}, u32[]{:S(2)}, u32[]{:S(2)}) async-start(bf16[32,32,256]{2,1,0:T(8,128)(2,1)} %pad_maximum_fusion), calls=%async_computation.1 | async-start | bytes 1048576 | tf_op jit(solution)/shard_map/all_to_all | solution.py:351
  37.6 1.1 copy-start.4
  38.8 28.6 %all-to-all-start.2 = ((bf16[16,384,128]{2,1,0:T(8,128)(2,1)}), bf16[16,384,128]{2,1,0:T(8,128)(2,1)S(1)}, u32[]{:S(2)}, u32[]{:S(2)}) async-start(bf16[16,384,128]{2,1,0:T(8,128)(2,1)} %bitcast.41), calls=%async_computation.2 | async-start | bytes 3145728 | tf_op jit(solution)/shard_map/all_to_all | solution.py:335
  55.5 1.4 copy-start.5
  58.0 1.2 copy-start.3
  67.4 1.2 copy-start.1
  67.4 8.8 %copy-start.7 = (f32[8]{0:T(128)S(1)}, f32[8]{0:T(128)}, u32[]{:S(2)}) copy-start(f32[8]{0:T(128)} %param.15) | copy-start | bytes 100
  68.5 28.4 %all-to-all-start.3 = ((bf16[16,384,128]{2,1,0:T(8,128)(2,1)}), bf16[16,384,128]{2,1,0:T(8,128)(2,1)}, u32[]{:S(2)}, u32[]{:S(2)}) async-start(bf16[16,384,128]{2,1,0:T(8,128)(2,1)} %bitcast.40), calls=%async_computation.3 | async-start | bytes 3145728 | tf_op jit(solution)/shard_map/all_to_all | solution.py:335
  77.3 1.4 copy-start.2
  108.5 42.1 %copy-start.6 = (s32[32,8]{0,1:T(8,128)S(1)}, s32[32,8]{0,1:T(8,128)}, u32[]{:S(2)}) copy-start(s32[32,8]{0,1:T(8,128)} %param.11) | copy-start | bytes 3076
  108.5 5.7 %collective-permute-start = (f32[264,128]{1,0:T(8,128)S(1)}, f32[264,128]{1,0:T(8,128)S(1)}, u32[]{:S(2)}, u32[]{:S(2)}) collective-permute-start(f32[264,128]{1,0:T(8,128)S(1)} %em_first.3.refs_0_), channel_id=1, source_target_pairs={{0,8},{8,16},{16,24},{24,0},{1,9},{9,17},{17,25},{25,1},{2,10},{10... | collective-permute-start | bytes 405512 | tf_op jit(solution)/shard_map/ppermute | solution.py:296
  108.6 8.2 %collective-permute-start.1 = (f32[264,128]{1,0:T(8,128)S(1)}, f32[264,128]{1,0:T(8,128)S(1)}, u32[]{:S(2)}, u32[]{:S(2)}) collective-permute-start(f32[264,128]{1,0:T(8,128)S(1)} %em_first.3.refs_0_), channel_id=1, source_target_pairs={{0,16},{8,24},{16,0},{24,8},{1,17},{9,25},{17,1},{25,9},{2,18},{10... | collective-permute-start | bytes 405512 | tf_op jit(solution)/shard_map/ppermute | solution.py:296
  112.9 5.4 %collective-permute-start.2 = (f32[264,128]{1,0:T(8,128)S(1)}, f32[264,128]{1,0:T(8,128)S(1)}, u32[]{:S(2)}, u32[]{:S(2)}) collective-permute-start(f32[264,128]{1,0:T(8,128)S(1)} %em_first.3.refs_0_), channel_id=1, source_target_pairs={{0,24},{8,0},{16,8},{24,16},{1,25},{9,1},{17,9},{25,17},{2,26},{10... | collective-permute-start | bytes 405512 | tf_op jit(solution)/shard_map/ppermute | solution.py:296
  131.7 14.5 %collective-permute-start.3 = (f32[264,128]{1,0:T(8,128)S(1)}, f32[264,128]{1,0:T(8,128)S(1)}, u32[]{:S(2)}, u32[]{:S(2)}) collective-permute-start(f32[264,128]{1,0:T(8,128)S(1)} %get-tuple-element.15.p0), channel_id=1, source_target_pairs={{0,8},{8,16},{16,24},{24,0},{1,9},{9,17},{17,25},{25,1},{2,10},{10... | collective-permute-start | bytes 405512 | tf_op jit(solution)/shard_map/ppermute | solution.py:296
  132.3 13.9 %collective-permute-start.4 = (f32[264,128]{1,0:T(8,128)S(1)}, f32[264,128]{1,0:T(8,128)S(1)}, u32[]{:S(2)}, u32[]{:S(2)}) collective-permute-start(f32[264,128]{1,0:T(8,128)S(1)} %get-tuple-element.15.p0), channel_id=1, source_target_pairs={{0,16},{8,24},{16,0},{24,8},{1,17},{9,25},{17,1},{25,9},{2,18},{10... | collective-permute-start | bytes 405512 | tf_op jit(solution)/shard_map/ppermute | solution.py:296
  135.0 11.2 %collective-permute-start.5 = (f32[264,128]{1,0:T(8,128)S(1)}, f32[264,128]{1,0:T(8,128)S(1)}, u32[]{:S(2)}, u32[]{:S(2)}) collective-permute-start(f32[264,128]{1,0:T(8,128)S(1)} %get-tuple-element.15.p0), channel_id=1, source_target_pairs={{0,24},{8,0},{16,8},{24,16},{1,25},{9,1},{17,9},{25,17},{2,26},{10... | collective-permute-start | bytes 405512 | tf_op jit(solution)/shard_map/ppermute | solution.py:296
  146.4 9.6 %collective-permute-start.6 = (f32[136,256]{1,0:T(8,128)S(1)}, f32[136,256]{1,0:T(8,128)S(1)}, u32[]{:S(2)}, u32[]{:S(2)}) collective-permute-start(f32[136,256]{1,0:T(8,128)S(1)} %update.1.x0), channel_id=1, source_target_pairs={{0,32},{32,64},{64,96},{96,0},{1,33},{33,65},{65,97},{97,1},{2,34}... | collective-permute-start | bytes 417800 | tf_op jit(solution)/shard_map/ppermute | solution.py:296
  147.4 8.7 %collective-permute-start.7 = (f32[136,256]{1,0:T(8,128)S(1)}, f32[136,256]{1,0:T(8,128)S(1)}, u32[]{:S(2)}, u32[]{:S(2)}) collective-permute-start(f32[136,256]{1,0:T(8,128)S(1)} %update.1.x0), channel_id=1, source_target_pairs={{0,64},{32,96},{64,0},{96,32},{1,65},{33,97},{65,1},{97,33},{2,66}... | collective-permute-start | bytes 417800 | tf_op jit(solution)/shard_map/ppermute | solution.py:296
  149.3 7.3 %collective-permute-start.8 = (f32[136,256]{1,0:T(8,128)S(1)}, f32[136,256]{1,0:T(8,128)S(1)}, u32[]{:S(2)}, u32[]{:S(2)}) collective-permute-start(f32[136,256]{1,0:T(8,128)S(1)} %update.1.x0), channel_id=1, source_target_pairs={{0,96},{32,0},{64,32},{96,64},{1,97},{33,1},{65,33},{97,65},{2,98}... | collective-permute-start | bytes 417800 | tf_op jit(solution)/shard_map/ppermute | solution.py:296

commit v5 on v4

--- a/solution.py
+++ b/solution.py
@@ -15,7 +15,7 @@
 NT = (((1,), (1,)), ((), ()))
 NN = (((1,), (0,)), ((), ()))
 WINDOW = 32
-TILE = 1024
+TILE = 2048
 CAP = 384
 
 

time: 158 us -> 157 us (level)
  Pallas kernels: 43.1 us -> 41.4 us
    pallas_call x3, Pallas kernels: 25.4 us -> 23.7 us  [em(): pl.pallas_call(functools.partial(em_kernel, halves, carried, last), out_s...]
  transfers between devices with their start and end apart: 13 -> 13, of which waited for: 8 -> 8; matrix products, arithmetic and copies ran while one was open for 15% -> 15% of each run, Pallas kernels for 10% -> 9%
where the time goes in v5:
time: 157 us; the launch traced here: 156 us
  starting transfers between devices  42.2 us (27%)
  Pallas kernels  41.4 us (26%)
  waiting for transfers between devices  32.3 us (21%)
  local copies, waits for them, and re-layouts  27.5 us (18%)
  blocking collectives  9.5 us (6%)
  other arithmetic  2.49 us (2%)
    pallas_call x3, Pallas kernels, em(): pl.pallas_call(functools.partial(em_kernel, halves, carried, last), out_s...  23.7 us
    gather x2, local copies, waits for them, and re-layouts, fetch(): found = centroids.at[want.reshape(4 * CAP)].get(mode='promise_in_bounds')  19.3 us
    all_to_all x2, waiting for transfers between devices, fetch(): lax.all_to_all(found.reshape(16, CAP, 128), ('z', 'y'), 0, 0, tiled=True)  16.1 us
    all_to_all x2, starting transfers between devices, fetch(): lax.all_to_all(found.reshape(16, CAP, 128), ('z', 'y'), 0, 0, tiled=True)  14.3 us
    ppermute x9, starting transfers between devices, shifts(): return [x] + [lax.ppermute(x, axis, turn(d)) for d in (1, 2, 3)]  13.5 us
    ppermute x9, waiting for transfers between devices, shifts(): return [x] + [lax.ppermute(x, axis, turn(d)) for d in (1, 2, 3)]  11.4 us
    all_to_all x1, starting transfers between devices, per_device(): lax.all_to_all(posting, ('z', 'y', 'sub'), 0, 0, tiled=True)  10.4 us
    pallas_call x2, Pallas kernels, select(): pl.pallas_call(functools.partial(select_kernel, half), out_shape=jax.Shap...  10.4 us
  transfers between devices with their start and end apart: 13, of which 8 were waited for; matrix products, arithmetic and copies ran while one was open for 15% of the time, Pallas kernels for 9%

profile of v5, /device:TPU:8, one launch (start us, length us, event | category | flops | bytes accessed | tf_op | source)
XLA Modules:
  0.0 156.4 jit_solution(4419559632701638645)
XLA Ops:
  0.6 1.6 send.1
  2.2 10.4 %all-to-all-start = ((s32[128,2,128]{2,1,0:T(2,128)}), s32[128,2,128]{2,1,0:T(2,128)S(1)}, u32[]{:S(2)}, u32[]{:S(2)}) async-start(s32[128,2,128]{2,1,0:T(2,128)} %send.1), calls=%async_computation | async-start | bytes 262144 | tf_op jit(solution)/shard_map/all_to_all | solution.py:313
  12.7 0.7 fusion.10
  13.4 0.2 fusion.1
  13.6 0.1 copy.26
  13.8 0.7 convert_multiply_fusion.1
  14.5 0.1 copy.27
  14.8 1.1 reshape.110
  15.9 0.1 copy.24
  16.0 0.9 pad_maximum_fusion
  16.9 4.8 %all-to-all-done = s32[128,2,128]{2,1,0:T(2,128)S(1)} async-done(((s32[128,2,128]{2,1,0:T(2,128)}), s32[128,2,128]{2,1,0:T(2,128)S(1)}, u32[]{:S(2)}, u32[]{:S(2)}) %all-to-all-start) | async-done | bytes 131104 | tf_op jit(solution)/shard_map/all_to_all | solution.py:313
  21.7 3.9 %all-to-all-start.1 = ((bf16[32,32,256]{2,1,0:T(8,128)(2,1)}), bf16[32,32,256]{2,1,0:T(8,128)(2,1)S(1)}, u32[]{:S(2)}, u32[]{:S(2)}) async-start(bf16[32,32,256]{2,1,0:T(8,128)(2,1)} %pad_maximum_fusion), calls=%async_computation.1 | async-start | bytes 1048576 | tf_op jit(solution)/shard_map/all_to_all | solution.py:351
  25.6 1.6 %lists.1 = (s32[4,384]{1,0:T(4,128)S(1)}, s32[4,384]{1,0:T(4,128)S(1)}) custom-call(s32[1]{0:T(128)} %bitcast.9.me_ref, s32[256,128]{1,0:T(8,128)S(1)} %bitcast.42), custom_call_target="tpu_custom_call" | custom-call | tf_op jit(solution)/shard_map/lists/pallas_call | solution.py:315
  27.2 9.3 %gather_fusion = bf16[1536,512]{1,0:T(8,128)(2,1)S(1)} fusion(bf16[8192,512]{1,0:T(8,128)(2,1)} %param.13, s32[2048]{0:T(1024)S(1)} %pad_clamp_fusion.1), kind=kCustom, calls=%fused_computation | custom fusion | bytes 3151872 | tf_op jit(solution)/shard_map/gather | solution.py:325
  36.6 1.1 split.2
  37.7 1.1 copy-done.4
  38.8 6.8 %all-to-all-start.2 = ((bf16[16,384,128]{2,1,0:T(8,128)(2,1)}), bf16[16,384,128]{2,1,0:T(8,128)(2,1)S(1)}, u32[]{:S(2)}, u32[]{:S(2)}) async-start(bf16[16,384,128]{2,1,0:T(8,128)(2,1)} %bitcast.41), calls=%async_computation.2 | async-start | bytes 3145728 | tf_op jit(solution)/shard_map/all_to_all | solution.py:335
  45.6 9.9 %gather_fusion.1 = bf16[1536,512]{1,0:T(8,128)(2,1)} fusion(bf16[8192,512]{1,0:T(8,128)(2,1)} %param.13, s32[2048]{0:T(1024)S(1)} %pad_clamp_fusion), kind=kCustom, calls=%fused_computation.1 | custom fusion | bytes 3151872 | tf_op jit(solution)/shard_map/gather | solution.py:325
  55.6 1.4 copy-done.5
  57.0 1.1 split.3
  58.0 1.2 copy-done.3
  59.2 8.2 %all-to-all-done.2.list_ref = bf16[16,384,128]{2,1,0:T(8,128)(2,1)S(1)} async-done(((bf16[16,384,128]{2,1,0:T(8,128)(2,1)}), bf16[16,384,128]{2,1,0:T(8,128)(2,1)S(1)}, u32[]{:S(2)}, u32[]{:S(2)}) %all-to-all-start.2) | async-done | bytes 1572896 | tf_op jit(solution)/shard_map/all_to_all | solution.py:335
  67.4 1.2 copy-done.1
  68.5 7.5 %all-to-all-start.3 = ((bf16[16,384,128]{2,1,0:T(8,128)(2,1)}), bf16[16,384,128]{2,1,0:T(8,128)(2,1)}, u32[]{:S(2)}, u32[]{:S(2)}) async-start(bf16[16,384,128]{2,1,0:T(8,128)(2,1)} %bitcast.40), calls=%async_computation.3 | async-start | bytes 3145728 | tf_op jit(solution)/shard_map/all_to_all | solution.py:335
  76.4 0.9 keys.1
  77.3 1.4 copy-done.2
  78.7 4.9 %select.2 = bf16[2,8,512,128]{3,2,1,0:T(8,128)(2,1)S(1)} custom-call(s32[32,128]{1,0:T(8,128)S(1)} %get-tuple-element.11.base_ref, f32[32,512]{1,0:T(8,128)S(1)} %get-tuple-element.12.key_ref, bf16[1024,256]{1,0:T(8,128)(2,1)S(1)} %bitcast.35, bf16[16,384,128]{2,1,0:T(8,128)(2,1)S(1)} %copy-done.2), custom_call_target="tpu_custom_call" | custom-call | tf_op jit(solution)/shard_map/select/pallas_call | solution.py:363
  83.6 5.4 %em_first.2.refs_0_ = f32[264,128]{1,0:T(8,128)S(1)} custom-call(bf16[2,4096,128]{2,1,0:T(8,128)(2,1)S(1)} %bitcast.31, bf16[1024,256]{1,0:T(8,128)(2,1)S(1)} %bitcast.36, f32[256,128]{1,0:T(8,128)S(1)} %copy.28.refs_2_.refs_3_.refs_7_, f32[1,128]{1,0:T(1,128)S(1)} %reshape_reshape.3.refs_3_.refs_4_.refs_8_), custom_call_target="tpu_custom_call" | custom-call | tf_op jit(solution)/shard_map/em_first/pallas_call | solution.py:259
  89.0 8.0 %all-to-all-done.3.list_ref = bf16[16,384,128]{2,1,0:T(8,128)(2,1)} async-done(((bf16[16,384,128]{2,1,0:T(8,128)(2,1)}), bf16[16,384,128]{2,1,0:T(8,128)(2,1)}, u32[]{:S(2)}, u32[]{:S(2)}) %all-to-all-start.3) | async-done | bytes 1572896 | tf_op jit(solution)/shard_map/all_to_all | solution.py:335
  97.0 5.5 %select.3 = bf16[2,8,512,128]{3,2,1,0:T(8,128)(2,1)S(1)} custom-call(s32[32,128]{1,0:T(8,128)S(1)} %get-tuple-element.11.base_ref, f32[32,512]{1,0:T(8,128)S(1)} %get-tuple-element.12.key_ref, bf16[1024,256]{1,0:T(8,128)(2,1)S(1)} %bitcast.37, bf16[16,384,128]{2,1,0:T(8,128)(2,1)} %all-to-all-done.3.list_ref), custom_call_target="tpu_custom_call" | custom-call | tf_op jit(solution)/shard_map/select/pallas_call | solution.py:363
  102.5 5.4 %em_first.3.refs_0_ = f32[264,128]{1,0:T(8,128)S(1)} custom-call(f32[264,128]{1,0:T(8,128)S(1)} %em_first.2.refs_0_, bf16[2,4096,128]{2,1,0:T(8,128)(2,1)S(1)} %bitcast.33, bf16[1024,256]{1,0:T(8,128)(2,1)S(1)} %bitcast.38, f32[256,128]{1,0:T(8,128)S(1)} %copy.28.refs_2_.refs_3_.refs_7_, f32[1,128]{1,0:T(1,128)S(1)} %reshape_reshape.3.refs_3_.refs_4_.refs_8_), custom_call_target="tpu_custom_call" | custom-call | tf_op jit(solution)/shard_map/em_first/pallas_call | solution.py:259
  107.9 0.1 collective-permute-start
  108.0 4.3 %collective-permute-start.1 = (f32[264,128]{1,0:T(8,128)S(1)}, f32[264,128]{1,0:T(8,128)S(1)}, u32[]{:S(2)}, u32[]{:S(2)}) collective-permute-start(f32[264,128]{1,0:T(8,128)S(1)} %em_first.3.refs_0_), channel_id=1, source_target_pairs={{0,16},{8,24},{16,0},{24,8},{1,17},{9,25},{17,1},{25,9},{2,18},{10... | collective-permute-start | bytes 405512 | tf_op jit(solution)/shard_map/ppermute | solution.py:296
  112.2 1.4 collective-permute-done.refs_1_
  113.6 2.6 %collective-permute-done.1.refs_2_ = f32[264,128]{1,0:T(8,128)S(1)} collective-permute-done((f32[264,128]{1,0:T(8,128)S(1)}, f32[264,128]{1,0:T(8,128)S(1)}, u32[]{:S(2)}, u32[]{:S(2)}) %collective-permute-start.1) | collective-permute-done | bytes 135200 | tf_op jit(solution)/shard_map/ppermute | solution.py:296
  116.2 1.4 collective-permute-done.2.refs_3_
  117.6 13.0 %em_last.1 = (f32[264,128]{1,0:T(8,128)S(1)}, f32[256,128]{1,0:T(8,128)S(1)}, f32[8,8,128]{2,1,0:T(8,128)S(1)}) custom-call(f32[264,128]{1,0:T(8,128)S(1)} %em_first.3.refs_0_, f32[264,128]{1,0:T(8,128)S(1)} %collective-permute-done.refs_1_, f32[264,128]{1,0:T(8,128)S(1)} %collective-permute-done.1.refs_2_, f32[264,128]{1,0:T(8,128)S(1)} %collective-permute-done.2.refs_3_, ...), custom_call_target="tpu_custom_call" | custom-call | tf_op jit(solution)/shard_map/em_last/pallas_call | solution.py:259
  130.6 0.6 collective-permute-start.3
  131.2 2.7 %collective-permute-start.4 = (f32[264,128]{1,0:T(8,128)S(1)}, f32[264,128]{1,0:T(8,128)S(1)}, u32[]{:S(2)}, u32[]{:S(2)}) collective-permute-start(f32[264,128]{1,0:T(8,128)S(1)} %get-tuple-element.15.p0), channel_id=1, source_target_pairs={{0,16},{8,24},{16,0},{24,8},{1,17},{9,25},{17,1},{25,9},{2,18},{10... | collective-permute-start | bytes 405512 | tf_op jit(solution)/shard_map/ppermute | solution.py:296
  133.9 1.7 %collective-permute-start.5 = (f32[264,128]{1,0:T(8,128)S(1)}, f32[264,128]{1,0:T(8,128)S(1)}, u32[]{:S(2)}, u32[]{:S(2)}) collective-permute-start(f32[264,128]{1,0:T(8,128)S(1)} %get-tuple-element.15.p0), channel_id=1, source_target_pairs={{0,24},{8,0},{16,8},{24,16},{1,25},{9,1},{17,9},{25,17},{2,26},{10... | collective-permute-start | bytes 405512 | tf_op jit(solution)/shard_map/ppermute | solution.py:296
  135.6 9.5 %all_to_all.25.err_ref = f32[8,8,128]{2,1,0:T(8,128)S(1)} all-to-all(f32[8,8,128]{2,1,0:T(8,128)S(1)} %get-tuple-element.17), channel_id=1, replica_groups=mesh['z'=4,'y'=4,'sub'=8] {'sub'}, dimensions={0} | all-to-all | bytes 65536 | tf_op jit(solution)/shard_map/all_to_all | solution.py:379
  145.1 0.2 update.1.x0
  145.3 1.0 collective-permute-start.6
  146.3 1.9 %collective-permute-start.7 = (f32[136,256]{1,0:T(8,128)S(1)}, f32[136,256]{1,0:T(8,128)S(1)}, u32[]{:S(2)}, u32[]{:S(2)}) collective-permute-start(f32[136,256]{1,0:T(8,128)S(1)} %update.1.x0), channel_id=1, source_target_pairs={{0,64},{32,96},{64,0},{96,32},{1,65},{33,97},{65,1},{97,33},{2,66}... | collective-permute-start | bytes 417800 | tf_op jit(solution)/shard_map/ppermute | solution.py:296
  148.2 1.3 collective-permute-start.8
  149.5 5.4 %collective-permute-done.6.x1 = f32[136,256]{1,0:T(8,128)S(1)} collective-permute-done((f32[136,256]{1,0:T(8,128)S(1)}, f32[136,256]{1,0:T(8,128)S(1)}, u32[]{:S(2)}, u32[]{:S(2)}) %collective-permute-start.6) | collective-permute-done | bytes 139296 | tf_op jit(solution)/shard_map/ppermute | solution.py:296
  155.0 0.6 collective-permute-done.8.x3
  155.5 0.8 assemble.1
  (37 shorter events, 0.8 us)
Async XLA Ops:
  0.6 75.4 %copy-start = (f32[8,256,64]{1,2,0:T(8,128)S(1)}, f32[8,256,64]{1,2,0:T(8,128)}, u32[]{:S(2)}) copy-start(f32[8,256,64]{1,2,0:T(8,128)} %param.14) | copy-start | bytes 1572868
  2.2 19.5 %all-to-all-start = ((s32[128,2,128]{2,1,0:T(2,128)}), s32[128,2,128]{2,1,0:T(2,128)S(1)}, u32[]{:S(2)}, u32[]{:S(2)}) async-start(s32[128,2,128]{2,1,0:T(2,128)} %send.1), calls=%async_computation | async-start | bytes 262144 | tf_op jit(solution)/shard_map/all_to_all | solution.py:313
  21.7 17.1 %all-to-all-start.1 = ((bf16[32,32,256]{2,1,0:T(8,128)(2,1)}), bf16[32,32,256]{2,1,0:T(8,128)(2,1)S(1)}, u32[]{:S(2)}, u32[]{:S(2)}) async-start(bf16[32,32,256]{2,1,0:T(8,128)(2,1)} %pad_maximum_fusion), calls=%async_computation.1 | async-start | bytes 1048576 | tf_op jit(solution)/shard_map/all_to_all | solution.py:351
  37.6 1.1 copy-start.4
  38.8 28.6 %all-to-all-start.2 = ((bf16[16,384,128]{2,1,0:T(8,128)(2,1)}), bf16[16,384,128]{2,1,0:T(8,128)(2,1)S(1)}, u32[]{:S(2)}, u32[]{:S(2)}) async-start(bf16[16,384,128]{2,1,0:T(8,128)(2,1)} %bitcast.41), calls=%async_computation.2 | async-start | bytes 3145728 | tf_op jit(solution)/shard_map/all_to_all | solution.py:335
  55.5 1.4 copy-start.5
  58.0 1.2 copy-start.3
  67.4 1.2 copy-start.1
  67.4 8.8 %copy-start.7 = (f32[8]{0:T(128)S(1)}, f32[8]{0:T(128)}, u32[]{:S(2)}) copy-start(f32[8]{0:T(128)} %param.15) | copy-start | bytes 100
  68.5 28.4 %all-to-all-start.3 = ((bf16[16,384,128]{2,1,0:T(8,128)(2,1)}), bf16[16,384,128]{2,1,0:T(8,128)(2,1)}, u32[]{:S(2)}, u32[]{:S(2)}) async-start(bf16[16,384,128]{2,1,0:T(8,128)(2,1)} %bitcast.40), calls=%async_computation.3 | async-start | bytes 3145728 | tf_op jit(solution)/shard_map/all_to_all | solution.py:335
  77.3 1.4 copy-start.2
  107.9 41.7 %copy-start.6 = (s32[32,8]{0,1:T(8,128)S(1)}, s32[32,8]{0,1:T(8,128)}, u32[]{:S(2)}) copy-start(s32[32,8]{0,1:T(8,128)} %param.11) | copy-start | bytes 3076
  107.9 5.7 %collective-permute-start = (f32[264,128]{1,0:T(8,128)S(1)}, f32[264,128]{1,0:T(8,128)S(1)}, u32[]{:S(2)}, u32[]{:S(2)}) collective-permute-start(f32[264,128]{1,0:T(8,128)S(1)} %em_first.3.refs_0_), channel_id=1, source_target_pairs={{0,8},{8,16},{16,24},{24,0},{1,9},{9,17},{17,25},{25,1},{2,10},{10... | collective-permute-start | bytes 405512 | tf_op jit(solution)/shard_map/ppermute | solution.py:296
  108.0 8.2 %collective-permute-start.1 = (f32[264,128]{1,0:T(8,128)S(1)}, f32[264,128]{1,0:T(8,128)S(1)}, u32[]{:S(2)}, u32[]{:S(2)}) collective-permute-start(f32[264,128]{1,0:T(8,128)S(1)} %em_first.3.refs_0_), channel_id=1, source_target_pairs={{0,16},{8,24},{16,0},{24,8},{1,17},{9,25},{17,1},{25,9},{2,18},{10... | collective-permute-start | bytes 405512 | tf_op jit(solution)/shard_map/ppermute | solution.py:296
  112.2 5.4 %collective-permute-start.2 = (f32[264,128]{1,0:T(8,128)S(1)}, f32[264,128]{1,0:T(8,128)S(1)}, u32[]{:S(2)}, u32[]{:S(2)}) collective-permute-start(f32[264,128]{1,0:T(8,128)S(1)} %em_first.3.refs_0_), channel_id=1, source_target_pairs={{0,24},{8,0},{16,8},{24,16},{1,25},{9,1},{17,9},{25,17},{2,26},{10... | collective-permute-start | bytes 405512 | tf_op jit(solution)/shard_map/ppermute | solution.py:296
  130.6 14.5 %collective-permute-start.3 = (f32[264,128]{1,0:T(8,128)S(1)}, f32[264,128]{1,0:T(8,128)S(1)}, u32[]{:S(2)}, u32[]{:S(2)}) collective-permute-start(f32[264,128]{1,0:T(8,128)S(1)} %get-tuple-element.15.p0), channel_id=1, source_target_pairs={{0,8},{8,16},{16,24},{24,0},{1,9},{9,17},{17,25},{25,1},{2,10},{10... | collective-permute-start | bytes 405512 | tf_op jit(solution)/shard_map/ppermute | solution.py:296
  131.2 13.9 %collective-permute-start.4 = (f32[264,128]{1,0:T(8,128)S(1)}, f32[264,128]{1,0:T(8,128)S(1)}, u32[]{:S(2)}, u32[]{:S(2)}) collective-permute-start(f32[264,128]{1,0:T(8,128)S(1)} %get-tuple-element.15.p0), channel_id=1, source_target_pairs={{0,16},{8,24},{16,0},{24,8},{1,17},{9,25},{17,1},{25,9},{2,18},{10... | collective-permute-start | bytes 405512 | tf_op jit(solution)/shard_map/ppermute | solution.py:296
  133.9 11.2 %collective-permute-start.5 = (f32[264,128]{1,0:T(8,128)S(1)}, f32[264,128]{1,0:T(8,128)S(1)}, u32[]{:S(2)}, u32[]{:S(2)}) collective-permute-start(f32[264,128]{1,0:T(8,128)S(1)} %get-tuple-element.15.p0), channel_id=1, source_target_pairs={{0,24},{8,0},{16,8},{24,16},{1,25},{9,1},{17,9},{25,17},{2,26},{10... | collective-permute-start | bytes 405512 | tf_op jit(solution)/shard_map/ppermute | solution.py:296
  145.3 9.6 %collective-permute-start.6 = (f32[136,256]{1,0:T(8,128)S(1)}, f32[136,256]{1,0:T(8,128)S(1)}, u32[]{:S(2)}, u32[]{:S(2)}) collective-permute-start(f32[136,256]{1,0:T(8,128)S(1)} %update.1.x0), channel_id=1, source_target_pairs={{0,32},{32,64},{64,96},{96,0},{1,33},{33,65},{65,97},{97,1},{2,34}... | collective-permute-start | bytes 417800 | tf_op jit(solution)/shard_map/ppermute | solution.py:296
  146.3 8.7 %collective-permute-start.7 = (f32[136,256]{1,0:T(8,128)S(1)}, f32[136,256]{1,0:T(8,128)S(1)}, u32[]{:S(2)}, u32[]{:S(2)}) collective-permute-start(f32[136,256]{1,0:T(8,128)S(1)} %update.1.x0), channel_id=1, source_target_pairs={{0,64},{32,96},{64,0},{96,32},{1,65},{33,97},{65,1},{97,33},{2,66}... | collective-permute-start | bytes 417800 | tf_op jit(solution)/shard_map/ppermute | solution.py:296
  148.2 7.3 %collective-permute-start.8 = (f32[136,256]{1,0:T(8,128)S(1)}, f32[136,256]{1,0:T(8,128)S(1)}, u32[]{:S(2)}, u32[]{:S(2)}) collective-permute-start(f32[136,256]{1,0:T(8,128)S(1)} %update.1.x0), channel_id=1, source_target_pairs={{0,96},{32,0},{64,32},{96,64},{1,97},{33,1},{65,33},{97,65},{2,98}... | collective-permute-start | bytes 417800 | tf_op jit(solution)/shard_map/ppermute | solution.py:296
